TPU v7x, 256 devices: a whole 4x4x8 slice. The times are simulated.
256 devices in a mesh: dm: 32 (over y, x, z_lo), chan: 8 (over z_hi, core).
Axes of the slice: x: 4, y: 4, z: 8 (z_hi: 4, z_lo: 2; z = z_hi * 2 + z_lo), core: 2. Of those that a mesh axis runs over, the one named last changes fastest.
Arguments:
- phased: bfloat16 [32, 256, 2, 4096], P('dm', None, None, 'chan')
- filters: bfloat16 [64, 4096, 512], P('dm', 'chan'), may hold values from -0.375 to 0.375
- tap_blocks: int32 [64], replicated, may hold values from 1 to 4, as said below
- stretch_owner: int32 [4], replicated, may hold values from 0 to 31, as said below
Outputs:
- normalized_power: float32 [64, 64, 4096], P('dm', None, 'chan')
Inputs may be any that keep to these rules, and one draw needn't show every extreme that they name: `stretch_owner`: the owners of the 4 stretches are distinct slots. `tap_blocks`: never falls from one trial to the next.
All inputs are finite; a program needn't handle non-finite values.
Results may differ from a plain program's by a relative error of at most 0.0003.
Values may be sent and summed in bfloat16 or wider, within the bound.
No kernel may reach another device: no remote copies, remote signals or barrier semaphores. Data moves between devices by JAX's collectives and lax.ppermute only.
A program may use at most 128 MiB of HBM per device.

v0:
```python
import jax
import jax.numpy as jnp
from jax import lax
from jax.sharding import PartitionSpec as P

CHANS = 4096
BLOCK = 64
STRETCHES = 4
DOWN = 16


epsilon = 1e-06


def spread(value, axis, source):
    kept = jnp.where(lax.axis_index(axis) == source, value, 0).astype(value.dtype)
    return lax.psum(kept, axis)


def masked_taps(tap_slab, tap_widths):
    tap_count = tap_slab.shape[2] // 2
    live = jnp.arange(tap_count, dtype=jnp.int32)[None, :] < tap_widths[:, None]
    live_both = jnp.concatenate([live, live], axis=1).astype(tap_slab.dtype)
    return tap_slab * live_both[:, None, :]


def build_kernel(tap_slab):
    tap_count = tap_slab.shape[2] // 2
    real_taps = tap_slab[:, :, :tap_count][:, :, ::-1]
    imag_taps = tap_slab[:, :, tap_count:][:, :, ::-1]
    from_real = jnp.stack([real_taps, imag_taps], axis=-1)
    from_imag = jnp.stack([-imag_taps, real_taps], axis=-1)
    stacked = jnp.stack([from_real, from_imag], axis=2)
    return stacked.transpose(3, 1, 2, 0, 4).reshape(tap_count, 1, -1)


def make_signal(previous, arrived):
    extended = jnp.concatenate([previous, arrived], axis=0)
    groups = extended.shape[2]
    return extended.transpose(0, 2, 1).reshape(1, -1, groups * 2)


def conv_power(signal, kernel, span_taps):
    tap_count = kernel.shape[0]
    features = signal.shape[2]
    channel_count = features // 2
    offset = 1 + tap_count - span_taps
    filtered = lax.conv_general_dilated(
        signal[:, offset:, :],
        kernel,
        (1,),
        "VALID",
        dimension_numbers=("NWC", "WIO", "NWC"),
        feature_group_count=features,
        preferred_element_type=jnp.float32,
    )
    length = filtered.shape[1]
    filtered = filtered.reshape(length, channel_count, 2, -1, 2)
    combined = jnp.sum(filtered, axis=2)
    energy = jnp.sum(combined * combined, axis=3)
    return jnp.sum(energy.reshape(length // DOWN, DOWN, channel_count, -1), axis=1) / DOWN


def respond(signal, kernel):
    tap_count = kernel.shape[0]
    return conv_power(signal, kernel, tap_count)


def fetch_stretch(held_stretch, owner):
    return spread(held_stretch, "dm", owner)


def body(phased, filters, tap_blocks, stretch_owner):
    held_stretch = phased[0]
    trials_dev = filters.shape[0]
    chan_count = filters.shape[1]
    tap_count = filters.shape[2] // 2
    my_index = lax.axis_index("dm")
    widths = tap_blocks * BLOCK
    my_widths = lax.dynamic_slice_in_dim(widths, my_index * trials_dev, trials_dev)
    kernel = build_kernel(masked_taps(filters, my_widths))
    previous = jnp.zeros((tap_count, 2, chan_count), held_stretch.dtype)
    pieces = []
    for index in range(STRETCHES):
        arrived = fetch_stretch(held_stretch, stretch_owner[index])
        signal = make_signal(previous, arrived)
        pieces.append(respond(signal, kernel))
        previous = arrived
    detected = jnp.concatenate(pieces, axis=0).transpose(2, 0, 1)
    band_total = lax.psum(jnp.sum(detected, axis=2), "chan")
    band_mean = band_total / CHANS
    return detected / (band_mean[:, :, None] + epsilon)


def solution(mesh):
    in_specs = (P("dm", None, None, "chan"), P("dm", "chan", None), P(), P())
    out_specs = P("dm", None, "chan")
    return jax.shard_map(body, mesh=mesh, in_specs=in_specs, out_specs=out_specs, check_vma=False)
```

profile of v0, /device:TPU:1, one launch (start us, length us, event | category | flops | bytes accessed | tf_op | source)
XLA Modules:
  0.0 935.8 jit_solution(14666470473648306016)
XLA Ops:
  6.5 1.5 fusion.7
  10.6 3.8 fusion
  14.4 0.1 dynamic_slice.3
  14.5 0.1 iota_compare_fusion
  14.6 0.1 broadcast_multiply_fusion
  14.6 0.1 fusion.6
  14.7 1.7 rev.7
  16.4 1.7 rev.6
  18.1 0.2 maximum_bitcast_fusion.1
  18.3 0.2 maximum_bitcast_fusion
  18.5 3.5 copy.75
  22.0 2.7 reshape.101
  24.8 7.7 copy.77
  32.5 288.7 %all-reduce.4.cloned.1.call-done = (bf16[256,2,512]{2,1,0:T(2,128)(2,1)}, bf16[256,2,512]{2,1,0:T(2,128)(2,1)}, bf16[256,2,512]{2,1,0:T(2,128)(2,1)}, bf16[256,2,512]{2,1,0:T(2,128)(2,1)}) async-done(((bf16[256,2,512]{2,1,0:T(2,128)(2,1)}, bf16[256,2,512]{2,1,0:T(2,128)(2,1)}, bf16[256,2,512]{2,1,0:T(2,128)(2,1)}, bf16[256,2,512]{2,1,0:T(2,128)(2,1)}), (bf16[256,2,512]{2,1,0:T(2,128)(2,1)}, ...) | async-done | bytes 2097168 | tf_op jit(solution)/shard_map/psum | solution.py:17
  321.1 7.2 pad_bitcast_fusion
  328.4 2.1 copy.80
  330.5 0.4 reshape.104
  330.9 0.5 slice_bitcast_fusion.2
  331.4 2.9 copy.82
  334.3 110.0 %fusion.9 = f32[1,256,1024,4]{2,0,3,1:T(1,128)} fusion(bf16[1,511,1024,1]{2,0,3,1:T(2,128)(2,1)S(1)} %copy.82, bf16[256,1,1024,4]{2,1,3,0:T(2,128)(2,1)} %copy.77), kind=kOutput, calls=%fused_computation.43 | convolution fusion | flops 536870912 | bytes 7337984 | tf_op jit(solution)/shard_map/convolution.1
  444.3 10.9 %copy.84 = f32[1,256,1024,4]{1,2,3,0:T(8,128)} copy(f32[1,256,1024,4]{2,0,3,1:T(1,128)} %fusion.9) | data formatting | bytes 8388608 | tf_op jit(solution)/shard_map/convolution.1
  455.2 6.0 reshape.106
  461.2 7.2 reduce_sum.120
  468.3 0.2 multiply_reduce_fusion.2
  468.5 0.3 copy.85
  468.9 0.8 bitcast_reduce_fusion.2
  469.8 2.1 copy.73
  471.9 0.4 reshape.99
  472.3 0.5 slice_bitcast_fusion.3
  472.8 2.9 copy.76
  475.7 110.0 %fusion.8 = f32[1,256,1024,4]{2,0,3,1:T(1,128)} fusion(bf16[1,511,1024,1]{2,0,3,1:T(2,128)(2,1)S(1)} %copy.76, bf16[256,1,1024,4]{2,1,3,0:T(2,128)(2,1)} %copy.77), kind=kOutput, calls=%fused_computation.42 | convolution fusion | flops 536870912 | bytes 7337984 | tf_op jit(solution)/shard_map/convolution
  585.7 10.9 %copy.78 = f32[1,256,1024,4]{1,2,3,0:T(8,128)} copy(f32[1,256,1024,4]{2,0,3,1:T(1,128)} %fusion.8) | data formatting | bytes 8388608 | tf_op jit(solution)/shard_map/convolution
  596.6 6.0 reshape.102
  602.6 7.2 reduce_sum.117
  609.8 0.2 multiply_reduce_fusion.3
  610.0 0.3 copy.79
  610.3 0.8 bitcast_reduce_fusion.3
  611.2 0.0 copy-done.1
  611.2 2.1 copy.86
  613.3 0.4 reshape.108
  613.8 0.5 slice_bitcast_fusion.1
  614.2 2.9 copy.88
  617.1 110.0 %fusion.10 = f32[1,256,1024,4]{2,0,3,1:T(1,128)} fusion(bf16[1,511,1024,1]{2,0,3,1:T(2,128)(2,1)S(1)} %copy.88, bf16[256,1,1024,4]{2,1,3,0:T(2,128)(2,1)} %copy.77), kind=kOutput, calls=%fused_computation.44 | convolution fusion | flops 536870912 | bytes 7337984 | tf_op jit(solution)/shard_map/convolution.2
  727.1 10.9 %copy.90 = f32[1,256,1024,4]{1,2,3,0:T(8,128)} copy(f32[1,256,1024,4]{2,0,3,1:T(1,128)} %fusion.10) | data formatting | bytes 8388608 | tf_op jit(solution)/shard_map/convolution.2
  738.1 6.2 reshape.110
  744.3 7.2 reduce_sum.123
  751.4 0.2 multiply_reduce_fusion.1
  751.6 0.3 copy.91
  752.0 0.8 bitcast_reduce_fusion.1
  752.9 2.1 copy.92
  755.0 0.4 reshape.112
  755.4 0.5 slice_bitcast_fusion
  755.9 2.9 copy.94
  758.8 110.0 %fusion.11 = f32[1,256,1024,4]{2,0,3,1:T(1,128)} fusion(bf16[1,511,1024,1]{2,0,3,1:T(2,128)(2,1)S(1)} %copy.94, bf16[256,1,1024,4]{2,1,3,0:T(2,128)(2,1)} %copy.77), kind=kOutput, calls=%fused_computation.45 | convolution fusion | flops 536870912 | bytes 7337984 | tf_op jit(solution)/shard_map/convolution.3
  868.8 10.9 %copy.96 = f32[1,256,1024,4]{1,2,3,0:T(8,128)} copy(f32[1,256,1024,4]{2,0,3,1:T(1,128)} %fusion.11) | data formatting | bytes 8388608 | tf_op jit(solution)/shard_map/convolution.3
  879.7 6.0 reshape.114
  885.7 7.2 reduce_sum.126
  892.9 0.2 multiply_reduce_fusion
  893.1 0.3 copy.97
  893.4 0.2 bitcast_reduce_fusion
  893.6 0.2 copy-done.4
  894.0 0.1 fusion.5
  894.1 33.9 %psum.39 = f32[2,64]{1,0:T(2,128)S(1)} all-reduce(f32[2,64]{1,0:T(2,128)S(1)} %fusion.5), channel_id=1, replica_groups=mesh['dm'=32,'chan'=8] {'chan'}, use_global_device_ids=true, to_apply=%region_17.18 | all-reduce | flops 128 | bytes 1024 | tf_op jit(solution)/shard_map/psum | solution.py:90
  928.0 0.8 fusion.4
  (22 shorter events, 0.3 us)
Async XLA Ops:
  6.5 314.6 %all-reduce.4.cloned.1.call-start = ((), (), s32[]{:S(2)}) async-start(), calls=%async_computation | async-start | bytes 4194304 | tf_op jit(solution)/shard_map/psum | solution.py:17
  10.5 3.8 copy-start.7
  10.6 4.0 copy-start.3
  468.5 1.2 copy-start.2
  610.0 1.2 copy-start.1
  751.6 1.2 copy-start
  893.1 0.8 copy-start.4
  893.1 0.9 copy-start.5
  893.1 0.9 copy-start.6
Sparse Core Ops, SparseCore 0:
  14.5 306.6 all-reduce.3
where the time goes:
time: 946 us; the launch traced here: 936 us
  matrix products  440 us (47%)
  waiting for transfers between devices  289 us (31%)
  local copies, waits for them, and re-layouts  112 us (12%)
  other arithmetic  44.6 us (5%)
  blocking collectives  33.9 us (4%)
  between operations  16.5 us (2%)
    another operation x4, matrix products  440 us
    psum x1, waiting for transfers between devices, spread(): return lax.psum(kept, axis)  289 us
    another operation x12, local copies, waits for them, and re-layouts  57.1 us
    psum x1, blocking collectives, body(): band_total = lax.psum(jnp.sum(detected, axis=2), 'chan')  33.9 us
    reduce_sum x4, other arithmetic, conv_power(): combined = jnp.sum(filtered, axis=2)  28.7 us
    reshape x4, local copies, waits for them, and re-layouts, conv_power(): filtered = filtered.reshape(length, channel_count, 2, -1, 2)  24.1 us
  transfers between devices with their start and end apart: 1, of which 1 were waited for; matrix products, arithmetic and copies ran while one was open for 2% of the time, Pallas kernels for 0%

commit v1 on v0

v1 whole, which is shorter than its diff:
```python
import functools

import jax
import jax.numpy as jnp
import numpy as np
from jax import lax
from jax.experimental import pallas as pl
from jax.experimental.pallas import tpu as pltpu
from jax.sharding import PartitionSpec as P

CHANS = 4096
BLOCK = 64
DOWN = 16
HALF = 256
NC = 16
GROUP = 2
DM = 32

epsilon = 1e-06


def place(i):
    return i // 8, (i // 2) % 4, i % 2


def index(y, x, z):
    return ((y % 4) * 4 + x % 4) * 2 + z % 2


def hop(value, dy, dx, dz):
    pairs = []
    for i in range(DM):
        y, x, z = place(i)
        pairs.append((i, index(y + dy, x + dx, z + dz)))
    return lax.ppermute(value, "dm", pairs)


def time_order():
    table = np.zeros((512,), np.int32)
    for bh in range(2):
        for ri in range(2):
            for bl in range(8):
                for m in range(16):
                    k = ((bh * 2 + ri) * 8 + bl) * 16 + m
                    table[k] = (16 * m + 15 - (8 * bh + bl)) * 2 + ri
    return table


def piece_table():
    rows = []
    for i in range(DM):
        y, x, _ = place(i)
        row = []
        for dy in (0, -1, 1, 2):
            for dx in (0, -1, 1, 2):
                row.append(4 * ((y + dy) % 4) + (x + dx) % 4)
        rows.append(row)
    return np.array(rows, np.int32)


TAP_CH = 16


def tap_kernel(width_ref, f_ref, o_ref):
    lane = lax.broadcasted_iota(jnp.int32, (16, 128), 1)
    row = lax.broadcasted_iota(jnp.int32, (16, 128), 0)
    keep = lane >= row

    def group(step, carry):
        at = pl.multiple_of(step * TAP_CH, TAP_CH)
        for t in range(2):
            live = width_ref[t]
            for h in range(2):
                block = f_ref[t, pl.ds(at, TAP_CH), 256 * h : 256 * h + 256].astype(jnp.float32)
                tap = lax.broadcasted_iota(jnp.int32, block.shape, 1)
                block = jnp.where(tap < live, block, 0.0)
                base = (t * 2 + h) * 16
                for c in range(TAP_CH):
                    low = jnp.broadcast_to(block[c : c + 1, :128], (16, 128))
                    high = jnp.broadcast_to(block[c : c + 1, 128:], (16, 128))
                    low = pltpu.roll(low, 0, 1, stride=1, stride_axis=0)
                    high = pltpu.roll(high, 0, 1, stride=1, stride_axis=0)
                    rows = slice(base, base + 16)
                    o_ref[at + c, rows, 0:128] = jnp.where(keep, low, 0.0).astype(jnp.bfloat16)
                    o_ref[at + c, rows, 128:256] = jnp.where(keep, high, low).astype(jnp.bfloat16)
                    o_ref[at + c, rows, 256:384] = jnp.where(keep, 0.0, high).astype(jnp.bfloat16)
        return carry

    lax.fori_loop(0, HALF // TAP_CH, group, 0)


def in_vmem():
    return pl.BlockSpec(memory_space=pltpu.VMEM)


def in_smem():
    return pl.BlockSpec(memory_space=pltpu.SMEM)


def build_taps(widths, taps):
    return pl.pallas_call(
        tap_kernel,
        in_specs=[in_smem(), in_vmem()],
        out_specs=in_vmem(),
        out_shape=jax.ShapeDtypeStruct((HALF, 64, 384), jnp.bfloat16),
        cost_estimate=pl.CostEstimate(flops=10_000_000, bytes_accessed=14_000_000, transcendentals=0),
        compiler_params=pltpu.CompilerParams(vmem_limit_bytes=16 << 20),
        name="build_taps",
    )(widths, taps)


def assemble_kernel(own_ref, x_ref, o_ref, scr):
    lane = lax.broadcasted_iota(jnp.int32, (16, 128), 1) // 16
    for bh in range(2):
        held = []
        for ri in range(2):
            for k in range(4):
                at = 256 * bh + 128 * ri
                held.append(x_ref[own_ref[k], :, at : at + 128].astype(jnp.float32))
        for k in (4, 2, 1):
            low = (lane & k) == 0
            for p in range(8):
                if p & k:
                    continue
                a, b = held[p], held[p + k]
                held[p] = jnp.where(low, a, pltpu.roll(b, 16 * k, 1))
                held[p + k] = jnp.where(low, pltpu.roll(a, 128 - 16 * k, 1), b)
        for bl in range(8):
            scr[pl.ds(8 * bh + bl, 16, stride=16), :] = held[bl]
    o_ref[...] = scr[...].reshape(16, 16, 128).astype(jnp.bfloat16)


def assemble(owner, arrived):
    return pl.pallas_call(
        assemble_kernel,
        in_specs=[in_smem(), in_vmem()],
        out_specs=in_vmem(),
        out_shape=jax.ShapeDtypeStruct((16, 16, 128), jnp.bfloat16),
        scratch_shapes=[pltpu.VMEM((256, 128), jnp.float32)],
        compiler_params=pltpu.CompilerParams(vmem_limit_bytes=16 << 20),
        name="assemble",
    )(owner, arrived)


def fold(rows):
    sub = lax.broadcasted_iota(jnp.int32, (8, 128), 0)
    for k in (4, 2, 1):
        low = (sub & k) == 0
        rows = [
            jnp.where(low, rows[i], rows[i + k])
            + jnp.where(low, pltpu.roll(rows[i], 8 - k, 0), pltpu.roll(rows[i + k], k, 0))
            for i in range(k)
        ]
    return rows[0]


def detect_kernel(counts, piece_ref, t0_ref, t1_ref, *rest):
    d_ref, b_ref, w_scr = rest[-3:]
    lane = lax.broadcasted_iota(jnp.int32, (16, 128), 1)
    inner = lane % 64
    sign = jnp.where(lane < 64, -1.0, 1.0)
    b_ref[...] = jnp.zeros_like(b_ref)

    def group(x_ref, first, step, carry):
        for p in range(GROUP):
            source = (step * GROUP + p) * NC
            base = pl.multiple_of(piece_ref[first + step * GROUP + p] * NC, NC)
            sums = [[] for _ in range(4)]
            for c in range(NC):
                x = x_ref[source + c]
                slot = p * NC + c
                w_scr[slot, 0:16, :] = x
                for a in range(1, 17):
                    moved = pltpu.roll(x, a, 1)
                    w_scr[slot, 16 * a : 16 * a + 16, :] = jnp.where(inner >= a, moved, jnp.zeros_like(x))
                taps = jnp.concatenate([t0_ref[base + c, :, :272], t1_ref[base + c, :, :272]], axis=0)
                out = jnp.dot(taps, w_scr[slot], preferred_element_type=jnp.float32)
                for t in range(4):
                    real = out[32 * t : 32 * t + 16]
                    imag = out[32 * t + 16 : 32 * t + 32]
                    y = real + sign * pltpu.roll(imag, 64, 1)
                    y = y * y
                    sums[t].append(y[:8] + y[8:])
            for t in range(4):
                for g in range(0, NC, 8):
                    total = fold(sums[t][g : g + 8])
                    total = (total + pltpu.roll(total, 64, 1)) * (1.0 / DOWN)
                    d_ref[t, pl.ds(base + g, 8)] = total
                    b_ref[t] += total
        return carry

    first = 0
    for x_ref, count in zip(rest, counts):
        lax.fori_loop(0, count // GROUP, functools.partial(group, x_ref, first), 0)
        first += count


def detect(pieces, samples, taps, earlier=None):
    counts = [part.shape[0] // NC for part in samples]
    n = sum(counts) * NC
    in_specs = [in_smem()] + [in_vmem()] * (2 + len(samples))
    args = [pieces, *taps, *samples]
    aliases = {}
    if earlier is not None:
        in_specs.append(in_vmem())
        args.append(earlier)
        aliases = {len(args) - 1: 0}
    return pl.pallas_call(
        functools.partial(detect_kernel, counts),
        in_specs=in_specs,
        out_specs=[in_vmem(), in_vmem()],
        out_shape=[
            jax.ShapeDtypeStruct((4, HALF, 128), jnp.float32),
            jax.ShapeDtypeStruct((4, 8, 128), jnp.float32),
        ],
        scratch_shapes=[pltpu.VMEM((GROUP * NC, 272, 128), jnp.bfloat16)],
        input_output_aliases=aliases,
        cost_estimate=pl.CostEstimate(
            flops=n * 128 * 512 * 128 * 2, bytes_accessed=n * 128 * 384 * 2, transcendentals=0
        ),
        compiler_params=pltpu.CompilerParams(vmem_limit_bytes=16 << 20),
        name="detect",
    )(*args)


def turn_kernel(d_ref, o_ref):
    for t in range(4):
        o_ref[t] = d_ref[t].T[:64]


def turn(detected):
    return pl.pallas_call(
        turn_kernel,
        in_specs=[in_vmem()],
        out_specs=in_vmem(),
        out_shape=jax.ShapeDtypeStruct((4, 64, HALF), jnp.float32),
        compiler_params=pltpu.CompilerParams(vmem_limit_bytes=16 << 20),
        name="turn",
    )(detected)


def body(phased, filters, tap_blocks, stretch_owner):
    me = lax.axis_index("dm")
    z = me % 2
    widths = tap_blocks * BLOCK
    mine = lax.dynamic_slice_in_dim(widths, me * 2, 2)
    partner = lax.dynamic_slice_in_dim(widths, (me + 1 - 2 * z) * 2, 2)
    pieces = lax.dynamic_index_in_dim(jnp.asarray(piece_table()), me, 0, keepdims=False)

    away = lax.dynamic_slice_in_dim(filters, (1 - z) * HALF, HALF, axis=1)
    partner_taps = hop(away, 0, 0, 1)
    stay = lax.dynamic_slice_in_dim(filters, z * HALF, HALF, axis=1)

    source = lax.broadcasted_iota(jnp.int32, (256, 2, 512), 0) * 2 + lax.broadcasted_iota(jnp.int32, (256, 2, 512), 1)
    order = (source == jnp.asarray(time_order())[None, None, :]).astype(jnp.bfloat16)
    held = jnp.einsum("trc,trk->ck", phased[0], order, preferred_element_type=jnp.float32).astype(jnp.bfloat16)
    sent = held.reshape(2, DM // 2, 16, 512).transpose(1, 0, 2, 3).reshape(DM, 16, 512)
    arrived = lax.all_to_all(sent, "dm", 0, 0, tiled=True)

    near = assemble(jnp.clip(stretch_owner, 0, DM - 1), arrived)
    stay, near = lax.optimization_barrier((stay, near))
    line = [hop(near, 0, k, 0) for k in (1, -1, 2)]
    taps0 = build_taps(mine, stay)
    taps0, *line = lax.optimization_barrier((taps0, *line))
    row = jnp.concatenate([near, *line], axis=0)
    taps = (taps0, build_taps(partner, partner_taps))
    low, high, far = hop(row, 1, 0, 0), hop(row, -1, 0, 0), hop(row, 2, 0, 0)

    detected, band0 = detect(pieces[:4], [row], taps)
    detected, band1 = detect(pieces[4:12], [low, high], taps, detected)
    detected, band2 = detect(pieces[12:], [far], taps, detected)

    band = jnp.sum(band0 + band1 + band2, axis=1)[:, :64]
    total = band[:2] + hop(band[2:], 0, 0, 1)
    turned = turn(detected)
    total, turned = lax.optimization_barrier((total, turned))
    other = hop(turned[2:], 0, 0, 1)
    total = total + lax.ppermute(total, "chan", [(i, i ^ 1) for i in range(8)])
    total, other = lax.optimization_barrier((total, other))
    total = total + lax.ppermute(total, "chan", [(i, i ^ 2) for i in range(8)])
    total = total + lax.ppermute(total, "chan", [(i, (6 - i // 2 * 2) + i % 2) for i in range(8)])

    own = turned[:2]
    low = jnp.where(z == 0, own, other)
    high = jnp.where(z == 0, other, own)
    power = jnp.concatenate([low, high], axis=2)
    return power / (total[:, :, None] / CHANS + epsilon)


def solution(mesh):
    in_specs = (P("dm", None, None, "chan"), P("dm", "chan", None), P(), P())
    out_specs = P("dm", None, "chan")
    return jax.shard_map(body, mesh=mesh, in_specs=in_specs, out_specs=out_specs, check_vma=False)
```

time: 946 us -> 76.8 us (0.08)
  the two profiles are of different devices: /device:TPU:1 before, /device:TPU:2 now
where the time goes in v1:
time: 76.8 us; the launch traced here: 76.5 us
  starting transfers between devices  27.6 us (36%)
  waiting for transfers between devices  20.6 us (27%)
  Pallas kernels  20.5 us (27%)
  local copies, waits for them, and re-layouts  4.14 us (5%)
  other arithmetic  2.17 us (3%)
  matrix products  1.29 us (2%)
    pallas_call x3, Pallas kernels, detect(): pl.pallas_call(functools.partial(detect_kernel, counts), in_specs=in_spec...  11.7 us
    ppermute x9, starting transfers between devices, hop(): return lax.ppermute(value, 'dm', pairs)  10.3 us
    all_to_all x1, starting transfers between devices, body(): arrived = lax.all_to_all(sent, 'dm', 0, 0, tiled=True)  8.98 us
    ppermute x9, waiting for transfers between devices, hop(): return lax.ppermute(value, 'dm', pairs)  8.95 us
    pallas_call x2, Pallas kernels, build_taps(): pl.pallas_call(tap_kernel, in_specs=[in_smem(), in_vmem()], out_specs=in_...  7.85 us
    all_to_all x1, waiting for transfers between devices, body(): arrived = lax.all_to_all(sent, 'dm', 0, 0, tiled=True)  7.46 us
    ppermute x1, starting transfers between devices, body(): lax.ppermute(total, 'chan', [(i, 6 - i // 2 * 2 + i % 2) for i in range(8)])  5.04 us
    ppermute x1, starting transfers between devices, body(): total = total + lax.ppermute(total, 'chan', [(i, i ^ 2) for i in range(8)])  3.28 us
  transfers between devices with their start and end apart: 13, of which 8 were waited for; matrix products, arithmetic and copies ran while one was open for 5% of the time, Pallas kernels for 23%

profile of v1, /device:TPU:2, one launch (start us, length us, event | category | flops | bytes accessed | tf_op | source)
XLA Modules:
  0.0 76.5 jit_solution(4550676753058335101)
XLA Ops:
  0.0 0.0 copy-start
  0.0 1.0 %copy-done = bf16[1,256,2,512]{3,2,1,0:T(2,128)(2,1)S(1)} copy-done((bf16[1,256,2,512]{3,2,1,0:T(2,128)(2,1)S(1)}, bf16[1,256,2,512]{3,2,1,0:T(2,128)(2,1)}, u32[]{:S(2)}) %copy-start) | copy-done | bytes 524312
  1.0 1.3 %fusion = bf16[512,512]{0,1:T(8,128)(2,1)S(1)} fusion(bf16[256,2,512]{2,1,0:T(2,128)(2,1)S(1)} %bitcast.17, s32[512]{0:T(512)} %constant.48.clone, s32[256]{0:T(256)S(1)} %iota_multiply_fusion), kind=kOutput, calls=%fused_computation.1 | convolution fusion | flops 269221888 | bytes 1051648 | tf_op jit(solution)/shard_map/trc,trk->ck/dot_general | solution.py:256
  2.3 0.8 %copy.10 = bf16[2,16,16,512]{3,2,0,1:T(8,128)(2,1)} copy(bf16[2,16,16,512]{3,2,1,0:T(8,128)(2,1)S(1)} %bitcast.18) | data formatting | bytes 1048576 | tf_op jit(solution)/shard_map/reshape | solution.py:257
  3.2 9.0 %all-to-all-start = ((bf16[32,16,512]{2,1,0:T(8,128)(2,1)}), bf16[32,16,512]{2,1,0:T(8,128)(2,1)S(1)}, u32[]{:S(2)}, u32[]{:S(2)}) async-start(bf16[32,16,512]{2,1,0:T(8,128)(2,1)} %bitcast.6), calls=%async_computation | async-start | bytes 1048576 | tf_op jit(solution)/shard_map/all_to_all | solution.py:258
  12.2 1.3 %constant_dynamic-slice_fusion = (bf16[2,256,512]{2,1,0:T(8,128)(2,1)S(1)}, bf16[2,256,512]{2,1,0:T(8,128)(2,1)S(1)}) fusion(bf16[2,512,512]{2,1,0:T(8,128)(2,1)} %param.7, s32[]{:T(128)S(6)} %select_n.41, s32[]{:T(128)S(6)} %select_n.39), kind=kLoop, calls=%fused_computation.17 | loop fusion | bytes 2097160 | tf_op jit(solution)/shard_map/dynamic_slice | solution.py:250
  13.5 1.6 %collective-permute-start.3 = (bf16[2,256,512]{2,1,0:T(8,128)(2,1)S(1)}, bf16[2,256,512]{2,1,0:T(8,128)(2,1)S(1)}, u32[]{:S(2)}, u32[]{:S(2)}) collective-permute-start(bf16[2,256,512]{2,1,0:T(8,128)(2,1)S(1)} %get-tuple-element.37), channel_id=1, source_target_pairs={{0,8},{8,0},{16,24},{24,16},{32,40},{40,32},{48,56},{56,48},{64,72... | collective-permute-start | bytes 1572872 | tf_op jit(solution)/shard_map/ppermute | solution.py:35
  15.0 0.7 constant_dynamic-slice_fusion.2
  15.7 0.7 broadcast_multiply_fusion
  16.4 0.1 fusion.4
  16.4 0.7 broadcast_clamp_fusion.own_ref
  17.1 0.1 slice_bitcast_fusion.2
  17.2 7.5 %all-to-all-done.x_ref = bf16[32,16,512]{2,1,0:T(8,128)(2,1)S(1)} async-done(((bf16[32,16,512]{2,1,0:T(8,128)(2,1)}), bf16[32,16,512]{2,1,0:T(8,128)(2,1)S(1)}, u32[]{:S(2)}, u32[]{:S(2)}) %all-to-all-start) | async-done | bytes 524320 | tf_op jit(solution)/shard_map/all_to_all | solution.py:258
  24.6 0.8 %assemble.1 = bf16[16,16,128]{2,1,0:T(8,128)(2,1)S(1)} custom-call(s32[4]{0:T(128)S(1)} %broadcast_clamp_fusion.own_ref, bf16[32,16,512]{2,1,0:T(8,128)(2,1)S(1)} %all-to-all-done.x_ref), custom_call_target="tpu_custom_call" | custom-call | tf_op jit(solution)/shard_map/assemble/pallas_call | solution.py:134
  25.4 0.5 collective-permute-start.2
  26.0 1.7 %collective-permute-start.1 = (bf16[16,16,128]{2,1,0:T(8,128)(2,1)S(1)}, bf16[16,16,128]{2,1,0:T(8,128)(2,1)S(1)}, u32[]{:S(2)}, u32[]{:S(2)}) collective-permute-start(bf16[16,16,128]{2,1,0:T(8,128)(2,1)S(1)} %assemble.1), channel_id=1, source_target_pairs={{0,48},{8,56},{16,0},{24,8},{32,16},{40,24},{48,32},{56,40},{64,11... | collective-permute-start | bytes 196616 | tf_op jit(solution)/shard_map/ppermute | solution.py:35
  27.7 0.8 collective-permute-start
  28.4 3.9 %build_taps.2.t0_ref = bf16[256,64,384]{2,1,0:T(8,128)(2,1)S(1)} custom-call(s32[2]{0:T(128)S(1)} %get-tuple-element.44.width_ref, bf16[2,256,512]{2,1,0:T(8,128)(2,1)S(1)} %get-tuple-element.21.f_ref), custom_call_target="tpu_custom_call" | custom-call | flops 10000000 | bytes 14000000 | tf_op jit(solution)/shard_map/build_taps/pallas_call | solution.py:101
  32.4 0.0 collective-permute-done.2
  32.4 0.0 collective-permute-done.1
  32.4 0.1 collective-permute-done
  32.5 1.1 %collective-permute-start.5 = (bf16[64,16,128]{2,1,0:T(8,128)(2,1)S(1)}, bf16[64,16,128]{2,1,0:T(8,128)(2,1)S(1)}, u32[]{:S(2)}, u32[]{:S(2)}) collective-permute-start(bf16[64,16,128]{2,1,0:T(8,128)(2,1)S(1)} %constant_dynamic-update-slice_fusion.rest_0_), channel_id=1, source_target_pairs={{0,192},{8,200},{16,208},{24,216},{32,224},{40,232},{48,240},{56,2... | collective-permute-start | bytes 786440 | tf_op jit(solution)/shard_map/ppermute | solution.py:35
  33.7 1.0 %collective-permute-start.4 = (bf16[64,16,128]{2,1,0:T(8,128)(2,1)S(1)}, bf16[64,16,128]{2,1,0:T(8,128)(2,1)S(1)}, u32[]{:S(2)}, u32[]{:S(2)}) collective-permute-start(bf16[64,16,128]{2,1,0:T(8,128)(2,1)S(1)} %constant_dynamic-update-slice_fusion.rest_0_), channel_id=1, source_target_pairs={{0,64},{8,72},{16,80},{24,88},{32,96},{40,104},{48,112},{56,120},{... | collective-permute-start | bytes 786440 | tf_op jit(solution)/shard_map/ppermute | solution.py:35
  34.6 0.1 slice_bitcast_fusion.1.piece_ref
  34.7 0.0 collective-permute-done.3.f_ref
  34.7 3.9 %build_taps.3.t1_ref = bf16[256,64,384]{2,1,0:T(8,128)(2,1)S(1)} custom-call(s32[2]{0:T(128)S(1)} %get-tuple-element.43.width_ref, bf16[2,256,512]{2,1,0:T(8,128)(2,1)S(1)} %collective-permute-done.3.f_ref), custom_call_target="tpu_custom_call" | custom-call | flops 10000000 | bytes 14000000 | tf_op jit(solution)/shard_map/build_taps/pallas_call | solution.py:101
  38.6 1.4 %collective-permute-start.6 = (bf16[64,16,128]{2,1,0:T(8,128)(2,1)S(1)}, bf16[64,16,128]{2,1,0:T(8,128)(2,1)S(1)}, u32[]{:S(2)}, u32[]{:S(2)}) collective-permute-start(bf16[64,16,128]{2,1,0:T(8,128)(2,1)S(1)} %constant_dynamic-update-slice_fusion.rest_0_), channel_id=1, source_target_pairs={{0,128},{8,136},{16,144},{24,152},{32,160},{40,168},{48,176},{56,1... | collective-permute-start | bytes 786440 | tf_op jit(solution)/shard_map/ppermute | solution.py:35
  40.0 3.1 %detect.3 = (f32[4,256,128]{2,1,0:T(8,128)S(1)}, f32[4,8,128]{2,1,0:T(8,128)S(1)}) custom-call(s32[4]{0:T(128)S(1)} %get-tuple-element.41.piece_ref, bf16[256,64,384]{2,1,0:T(8,128)(2,1)S(1)} %build_taps.2.t0_ref, bf16[256,64,384]{2,1,0:T(8,128)(2,1)S(1)} %build_taps.3.t1_ref, bf16[64,16,128]{2,1,0:T(8,128)(2,1)S(1)} %constant_dynamic-update-slice_fusion.rest_0_), custom_call_target="tpu_custom_call" | custom-call | flops 1073741824 | bytes 6291456 | tf_op jit(solution)/shard_map/detect/pallas_call | solution.py:208
  43.1 0.0 collective-permute-done.5.rest_1_
  43.1 3.8 %collective-permute-done.4.rest_0_ = bf16[64,16,128]{2,1,0:T(8,128)(2,1)S(1)} collective-permute-done((bf16[64,16,128]{2,1,0:T(8,128)(2,1)S(1)}, bf16[64,16,128]{2,1,0:T(8,128)(2,1)S(1)}, u32[]{:S(2)}, u32[]{:S(2)}) %collective-permute-start.4) | collective-permute-done | bytes 262176 | tf_op jit(solution)/shard_map/ppermute | solution.py:35
  46.9 5.6 %detect.4 = (f32[4,256,128]{2,1,0:T(8,128)S(1)}, f32[4,8,128]{2,1,0:T(8,128)S(1)}) custom-call(s32[8]{0:T(128)S(1)} %slice_bitcast_fusion.1.piece_ref, bf16[256,64,384]{2,1,0:T(8,128)(2,1)S(1)} %build_taps.2.t0_ref, bf16[256,64,384]{2,1,0:T(8,128)(2,1)S(1)} %build_taps.3.t1_ref, ...), custom_call_target="tpu_custom_call", output_to_operand_aliasing={{0}: (5, {})} | custom-call | flops 2147483648 | bytes 12582912 | tf_op jit(solution)/shard_map/detect/pallas_call | solution.py:208
  52.4 0.0 collective-permute-done.6.rest_0_
  52.4 3.1 %detect.5 = (f32[4,256,128]{2,1,0:T(8,128)S(1)}, f32[4,8,128]{2,1,0:T(8,128)S(1)}) custom-call(s32[4]{0:T(128)S(1)} %get-tuple-element.42.piece_ref, bf16[256,64,384]{2,1,0:T(8,128)(2,1)S(1)} %build_taps.2.t0_ref, bf16[256,64,384]{2,1,0:T(8,128)(2,1)S(1)} %build_taps.3.t1_ref, ...), custom_call_target="tpu_custom_call", output_to_operand_aliasing={{0}: (4, {})} | custom-call | flops 1073741824 | bytes 6291456 | tf_op jit(solution)/shard_map/detect/pallas_call | solution.py:208
  55.5 1.1 %collective-permute-start.7 = (f32[2,64]{1,0:T(2,128)S(1)}, f32[2,64]{1,0:T(2,128)S(1)}, u32[]{:S(2)}, u32[]{:S(2)}) collective-permute-start(f32[2,64]{1,0:T(2,128)S(1)} %slice.40), channel_id=1, source_target_pairs={{0,8},{8,0},{16,24},{24,16},{32,40},{40,32},{48,56},{56,48},{64,72... | collective-permute-start | bytes 1544 | tf_op jit(solution)/shard_map/ppermute | solution.py:35
  56.7 0.2 turn.1
  56.9 2.3 %collective-permute-done.7 = f32[2,64]{1,0:T(2,128)S(1)} collective-permute-done((f32[2,64]{1,0:T(2,128)S(1)}, f32[2,64]{1,0:T(2,128)S(1)}, u32[]{:S(2)}, u32[]{:S(2)}) %collective-permute-start.7) | collective-permute-done | bytes 544 | tf_op jit(solution)/shard_map/ppermute | solution.py:35
  59.2 1.1 %collective-permute-start.9 = (f32[2,64,256]{2,1,0:T(8,128)S(1)}, f32[2,64,256]{2,1,0:T(8,128)S(1)}, u32[]{:S(2)}, u32[]{:S(2)}) collective-permute-start(f32[2,64,256]{2,1,0:T(8,128)S(1)} %slice.42), channel_id=1, source_target_pairs={{0,8},{8,0},{16,24},{24,16},{32,40},{40,32},{48,56},{56,48},{64,72... | collective-permute-start | bytes 393224 | tf_op jit(solution)/shard_map/ppermute | solution.py:35
  60.3 0.0 collective-permute-start.8
  60.4 1.1 %collective-permute-done.8 = f32[2,64]{1,0:T(2,128)S(1)} collective-permute-done((f32[2,64]{1,0:T(2,128)S(1)}, f32[2,64]{1,0:T(2,128)S(1)}, u32[]{:S(2)}, u32[]{:S(2)}) %collective-permute-start.8) | collective-permute-done | bytes 544 | tf_op jit(solution)/shard_map/ppermute | solution.py:278
  61.5 2.8 %collective-permute-done.9 = f32[2,64,256]{2,1,0:T(8,128)S(1)} collective-permute-done((f32[2,64,256]{2,1,0:T(8,128)S(1)}, f32[2,64,256]{2,1,0:T(8,128)S(1)}, u32[]{:S(2)}, u32[]{:S(2)}) %collective-permute-start.9) | collective-permute-done | bytes 131104 | tf_op jit(solution)/shard_map/ppermute | solution.py:35
  64.3 3.3 %collective-permute-start.10 = (f32[2,64]{1,0:T(2,128)S(1)}, f32[2,64]{1,0:T(2,128)S(1)}, u32[]{:S(2)}, u32[]{:S(2)}) collective-permute-start(f32[2,64]{1,0:T(2,128)S(1)} %add.62), channel_id=1, source_target_pairs={{0,2},{1,3},{2,0},{3,1},{4,6},{5,7},{6,4},{7,5},{8,10},{9,11},{10,... | collective-permute-start | bytes 1544 | tf_op jit(solution)/shard_map/ppermute | solution.py:280
  67.6 1.5 %collective-permute-done.10 = f32[2,64]{1,0:T(2,128)S(1)} collective-permute-done((f32[2,64]{1,0:T(2,128)S(1)}, f32[2,64]{1,0:T(2,128)S(1)}, u32[]{:S(2)}, u32[]{:S(2)}) %collective-permute-start.10) | collective-permute-done | bytes 544 | tf_op jit(solution)/shard_map/ppermute | solution.py:280
  69.1 5.0 %collective-permute-start.11 = (f32[2,64]{1,0:T(2,128)S(1)}, f32[2,64]{1,0:T(2,128)S(1)}, u32[]{:S(2)}, u32[]{:S(2)}) collective-permute-start(f32[2,64]{1,0:T(2,128)S(1)} %add.63), channel_id=1, source_target_pairs={{0,6},{1,7},{2,4},{3,5},{4,2},{5,3},{6,0},{7,1},{8,14},{9,15},{10,... | collective-permute-start | bytes 1544 | tf_op jit(solution)/shard_map/ppermute | solution.py:281
  74.2 1.5 %collective-permute-done.11 = f32[2,64]{1,0:T(2,128)S(1)} collective-permute-done((f32[2,64]{1,0:T(2,128)S(1)}, f32[2,64]{1,0:T(2,128)S(1)}, u32[]{:S(2)}, u32[]{:S(2)}) %collective-permute-start.11) | collective-permute-done | bytes 544 | tf_op jit(solution)/shard_map/ppermute | solution.py:281
  75.7 0.8 %maximum_divide_fusion = f32[2,64,512]{2,1,0:T(8,128)} fusion(f32[2,64,256]{2,1,0:T(8,128)S(1)} %get-tuple-element.40, f32[2,64,256]{2,1,0:T(8,128)S(1)} %get-tuple-element.39, f32[2,64]{1,0:T(2,128)S(1)} %multiply_add_fusion), kind=kLoop, calls=%fused_computation.6 | loop fusion | flops 131072 | bytes 524800 | tf_op jit(solution)/shard_map/div | solution.py:287
  (13 shorter events, 0.1 us)
Async XLA Ops:
  0.0 1.0 %copy-start = (bf16[1,256,2,512]{3,2,1,0:T(2,128)(2,1)S(1)}, bf16[1,256,2,512]{3,2,1,0:T(2,128)(2,1)}, u32[]{:S(2)}) copy-start(bf16[1,256,2,512]{3,2,1,0:T(2,128)(2,1)} %param.6) | copy-start | bytes 1572868
  3.2 21.5 %all-to-all-start = ((bf16[32,16,512]{2,1,0:T(8,128)(2,1)}), bf16[32,16,512]{2,1,0:T(8,128)(2,1)S(1)}, u32[]{:S(2)}, u32[]{:S(2)}) async-start(bf16[32,16,512]{2,1,0:T(8,128)(2,1)} %bitcast.6), calls=%async_computation | async-start | bytes 1048576 | tf_op jit(solution)/shard_map/all_to_all | solution.py:258
  13.5 21.2 %collective-permute-start.3 = (bf16[2,256,512]{2,1,0:T(8,128)(2,1)S(1)}, bf16[2,256,512]{2,1,0:T(8,128)(2,1)S(1)}, u32[]{:S(2)}, u32[]{:S(2)}) collective-permute-start(bf16[2,256,512]{2,1,0:T(8,128)(2,1)S(1)} %get-tuple-element.37), channel_id=1, source_target_pairs={{0,8},{8,0},{16,24},{24,16},{32,40},{40,32},{48,56},{56,48},{64,72... | collective-permute-start | bytes 1572872 | tf_op jit(solution)/shard_map/ppermute | solution.py:35
  25.4 7.0 %collective-permute-start.2 = (bf16[16,16,128]{2,1,0:T(8,128)(2,1)S(1)}, bf16[16,16,128]{2,1,0:T(8,128)(2,1)S(1)}, u32[]{:S(2)}, u32[]{:S(2)}) collective-permute-start(bf16[16,16,128]{2,1,0:T(8,128)(2,1)S(1)} %assemble.1), channel_id=1, source_target_pairs={{0,32},{8,40},{16,48},{24,56},{32,0},{40,8},{48,16},{56,24},{64,96... | collective-permute-start | bytes 196616 | tf_op jit(solution)/shard_map/ppermute | solution.py:35
  26.0 6.5 %collective-permute-start.1 = (bf16[16,16,128]{2,1,0:T(8,128)(2,1)S(1)}, bf16[16,16,128]{2,1,0:T(8,128)(2,1)S(1)}, u32[]{:S(2)}, u32[]{:S(2)}) collective-permute-start(bf16[16,16,128]{2,1,0:T(8,128)(2,1)S(1)} %assemble.1), channel_id=1, source_target_pairs={{0,48},{8,56},{16,0},{24,8},{32,16},{40,24},{48,32},{56,40},{64,11... | collective-permute-start | bytes 196616 | tf_op jit(solution)/shard_map/ppermute | solution.py:35
  27.7 4.8 %collective-permute-start = (bf16[16,16,128]{2,1,0:T(8,128)(2,1)S(1)}, bf16[16,16,128]{2,1,0:T(8,128)(2,1)S(1)}, u32[]{:S(2)}, u32[]{:S(2)}) collective-permute-start(bf16[16,16,128]{2,1,0:T(8,128)(2,1)S(1)} %assemble.1), channel_id=1, source_target_pairs={{0,16},{8,24},{16,32},{24,40},{32,48},{40,56},{48,0},{56,8},{64,80... | collective-permute-start | bytes 196616 | tf_op jit(solution)/shard_map/ppermute | solution.py:35
  32.5 10.6 %collective-permute-start.5 = (bf16[64,16,128]{2,1,0:T(8,128)(2,1)S(1)}, bf16[64,16,128]{2,1,0:T(8,128)(2,1)S(1)}, u32[]{:S(2)}, u32[]{:S(2)}) collective-permute-start(bf16[64,16,128]{2,1,0:T(8,128)(2,1)S(1)} %constant_dynamic-update-slice_fusion.rest_0_), channel_id=1, source_target_pairs={{0,192},{8,200},{16,208},{24,216},{32,224},{40,232},{48,240},{56,2... | collective-permute-start | bytes 786440 | tf_op jit(solution)/shard_map/ppermute | solution.py:35
  33.7 13.2 %collective-permute-start.4 = (bf16[64,16,128]{2,1,0:T(8,128)(2,1)S(1)}, bf16[64,16,128]{2,1,0:T(8,128)(2,1)S(1)}, u32[]{:S(2)}, u32[]{:S(2)}) collective-permute-start(bf16[64,16,128]{2,1,0:T(8,128)(2,1)S(1)} %constant_dynamic-update-slice_fusion.rest_0_), channel_id=1, source_target_pairs={{0,64},{8,72},{16,80},{24,88},{32,96},{40,104},{48,112},{56,120},{... | collective-permute-start | bytes 786440 | tf_op jit(solution)/shard_map/ppermute | solution.py:35
  38.6 13.8 %collective-permute-start.6 = (bf16[64,16,128]{2,1,0:T(8,128)(2,1)S(1)}, bf16[64,16,128]{2,1,0:T(8,128)(2,1)S(1)}, u32[]{:S(2)}, u32[]{:S(2)}) collective-permute-start(bf16[64,16,128]{2,1,0:T(8,128)(2,1)S(1)} %constant_dynamic-update-slice_fusion.rest_0_), channel_id=1, source_target_pairs={{0,128},{8,136},{16,144},{24,152},{32,160},{40,168},{48,176},{56,1... | collective-permute-start | bytes 786440 | tf_op jit(solution)/shard_map/ppermute | solution.py:35
  55.5 3.7 %collective-permute-start.7 = (f32[2,64]{1,0:T(2,128)S(1)}, f32[2,64]{1,0:T(2,128)S(1)}, u32[]{:S(2)}, u32[]{:S(2)}) collective-permute-start(f32[2,64]{1,0:T(2,128)S(1)} %slice.40), channel_id=1, source_target_pairs={{0,8},{8,0},{16,24},{24,16},{32,40},{40,32},{48,56},{56,48},{64,72... | collective-permute-start | bytes 1544 | tf_op jit(solution)/shard_map/ppermute | solution.py:35
  59.2 5.1 %collective-permute-start.9 = (f32[2,64,256]{2,1,0:T(8,128)S(1)}, f32[2,64,256]{2,1,0:T(8,128)S(1)}, u32[]{:S(2)}, u32[]{:S(2)}) collective-permute-start(f32[2,64,256]{2,1,0:T(8,128)S(1)} %slice.42), channel_id=1, source_target_pairs={{0,8},{8,0},{16,24},{24,16},{32,40},{40,32},{48,56},{56,48},{64,72... | collective-permute-start | bytes 393224 | tf_op jit(solution)/shard_map/ppermute | solution.py:35
  60.3 1.1 %collective-permute-start.8 = (f32[2,64]{1,0:T(2,128)S(1)}, f32[2,64]{1,0:T(2,128)S(1)}, u32[]{:S(2)}, u32[]{:S(2)}) collective-permute-start(f32[2,64]{1,0:T(2,128)S(1)} %slice_add_fusion), channel_id=1, source_target_pairs={{0,1},{1,0},{2,3},{3,2},{4,5},{5,4},{6,7},{7,6},{8,9},{9,8},{10,11... | collective-permute-start | bytes 1544 | tf_op jit(solution)/shard_map/ppermute | solution.py:278
  64.3 4.8 %collective-permute-start.10 = (f32[2,64]{1,0:T(2,128)S(1)}, f32[2,64]{1,0:T(2,128)S(1)}, u32[]{:S(2)}, u32[]{:S(2)}) collective-permute-start(f32[2,64]{1,0:T(2,128)S(1)} %add.62), channel_id=1, source_target_pairs={{0,2},{1,3},{2,0},{3,1},{4,6},{5,7},{6,4},{7,5},{8,10},{9,11},{10,... | collective-permute-start | bytes 1544 | tf_op jit(solution)/shard_map/ppermute | solution.py:280
  69.1 6.6 %collective-permute-start.11 = (f32[2,64]{1,0:T(2,128)S(1)}, f32[2,64]{1,0:T(2,128)S(1)}, u32[]{:S(2)}, u32[]{:S(2)}) collective-permute-start(f32[2,64]{1,0:T(2,128)S(1)} %add.63), channel_id=1, source_target_pairs={{0,6},{1,7},{2,4},{3,5},{4,2},{5,3},{6,0},{7,1},{8,14},{9,15},{10,... | collective-permute-start | bytes 1544 | tf_op jit(solution)/shard_map/ppermute | solution.py:281

commit v2 on v1

--- a/solution.py
+++ b/solution.py
@@ -13,7 +13,7 @@
 DOWN = 16
 HALF = 256
 NC = 16
-GROUP = 2
+GROUP = 4
 DM = 32
 
 epsilon = 1e-06
@@ -58,10 +58,10 @@
     return np.array(rows, np.int32)
 
 
-TAP_CH = 16
-
-
-def tap_kernel(width_ref, f_ref, o_ref):
+TAP_CH = 32
+
+
+def tap_kernel(live_ref, f_ref, o_ref, scr):
     lane = lax.broadcasted_iota(jnp.int32, (16, 128), 1)
     row = lax.broadcasted_iota(jnp.int32, (16, 128), 0)
     keep = lane >= row
@@ -69,18 +69,20 @@
     def group(step, carry):
         at = pl.multiple_of(step * TAP_CH, TAP_CH)
         for t in range(2):
-            live = width_ref[t]
+            block = f_ref[t, pl.ds(at, TAP_CH)].astype(jnp.float32)
+            tap = lax.broadcasted_iota(jnp.int32, block.shape, 1) % 256
+            block = jnp.where(tap < live_ref[t], block, 0.0)
+            for k in range(4):
+                scr[4 * t + k] = block[:, 128 * k : 128 * k + 128]
+        for t in range(2):
             for h in range(2):
-                block = f_ref[t, pl.ds(at, TAP_CH), 256 * h : 256 * h + 256].astype(jnp.float32)
-                tap = lax.broadcasted_iota(jnp.int32, block.shape, 1)
-                block = jnp.where(tap < live, block, 0.0)
                 base = (t * 2 + h) * 16
+                rows = slice(base, base + 16)
                 for c in range(TAP_CH):
-                    low = jnp.broadcast_to(block[c : c + 1, :128], (16, 128))
-                    high = jnp.broadcast_to(block[c : c + 1, 128:], (16, 128))
+                    low = scr[4 * t + 2 * h, pl.ds(c, 16, stride=0)]
+                    high = scr[4 * t + 2 * h + 1, pl.ds(c, 16, stride=0)]
                     low = pltpu.roll(low, 0, 1, stride=1, stride_axis=0)
                     high = pltpu.roll(high, 0, 1, stride=1, stride_axis=0)
-                    rows = slice(base, base + 16)
                     o_ref[at + c, rows, 0:128] = jnp.where(keep, low, 0.0).astype(jnp.bfloat16)
                     o_ref[at + c, rows, 128:256] = jnp.where(keep, high, low).astype(jnp.bfloat16)
                     o_ref[at + c, rows, 256:384] = jnp.where(keep, 0.0, high).astype(jnp.bfloat16)
@@ -103,6 +105,7 @@
         in_specs=[in_smem(), in_vmem()],
         out_specs=in_vmem(),
         out_shape=jax.ShapeDtypeStruct((HALF, 64, 384), jnp.bfloat16),
+        scratch_shapes=[pltpu.VMEM((8, TAP_CH, 128), jnp.float32)],
         cost_estimate=pl.CostEstimate(flops=10_000_000, bytes_accessed=14_000_000, transcendentals=0),
         compiler_params=pltpu.CompilerParams(vmem_limit_bytes=16 << 20),
         name="build_taps",
@@ -154,17 +157,17 @@
     return rows[0]
 
 
-def detect_kernel(counts, piece_ref, t0_ref, t1_ref, *rest):
+def detect_kernel(count, piece_ref, t0_ref, t1_ref, x_ref, *rest):
     d_ref, b_ref, w_scr = rest[-3:]
     lane = lax.broadcasted_iota(jnp.int32, (16, 128), 1)
     inner = lane % 64
     sign = jnp.where(lane < 64, -1.0, 1.0)
     b_ref[...] = jnp.zeros_like(b_ref)
 
-    def group(x_ref, first, step, carry):
+    def group(step, carry):
         for p in range(GROUP):
             source = (step * GROUP + p) * NC
-            base = pl.multiple_of(piece_ref[first + step * GROUP + p] * NC, NC)
+            base = pl.multiple_of(piece_ref[step * GROUP + p] * NC, NC)
             sums = [[] for _ in range(4)]
             for c in range(NC):
                 x = x_ref[source + c]
@@ -189,24 +192,20 @@
                     b_ref[t] += total
         return carry
 
-    first = 0
-    for x_ref, count in zip(rest, counts):
-        lax.fori_loop(0, count // GROUP, functools.partial(group, x_ref, first), 0)
-        first += count
+    lax.fori_loop(0, count // GROUP, group, 0)
 
 
 def detect(pieces, samples, taps, earlier=None):
-    counts = [part.shape[0] // NC for part in samples]
-    n = sum(counts) * NC
-    in_specs = [in_smem()] + [in_vmem()] * (2 + len(samples))
-    args = [pieces, *taps, *samples]
+    n = samples.shape[0]
+    in_specs = [in_smem()] + [in_vmem()] * 3
+    args = [pieces, *taps, samples]
     aliases = {}
     if earlier is not None:
         in_specs.append(in_vmem())
         args.append(earlier)
         aliases = {len(args) - 1: 0}
     return pl.pallas_call(
-        functools.partial(detect_kernel, counts),
+        functools.partial(detect_kernel, n // NC),
         in_specs=in_specs,
         out_specs=[in_vmem(), in_vmem()],
         out_shape=[
@@ -261,23 +260,24 @@
     stay, near = lax.optimization_barrier((stay, near))
     line = [hop(near, 0, k, 0) for k in (1, -1, 2)]
     taps0 = build_taps(mine, stay)
-    taps0, *line = lax.optimization_barrier((taps0, *line))
+    taps0, line = lax.optimization_barrier((taps0, line))
+    taps = (taps0, build_taps(partner, partner_taps))
     row = jnp.concatenate([near, *line], axis=0)
-    taps = (taps0, build_taps(partner, partner_taps))
     low, high, far = hop(row, 1, 0, 0), hop(row, -1, 0, 0), hop(row, 2, 0, 0)
 
-    detected, band0 = detect(pieces[:4], [row], taps)
-    detected, band1 = detect(pieces[4:12], [low, high], taps, detected)
-    detected, band2 = detect(pieces[12:], [far], taps, detected)
-
-    band = jnp.sum(band0 + band1 + band2, axis=1)[:, :64]
+    detected, bands = None, []
+    for step, part in enumerate((row, low, high, far)):
+        detected, band = detect(pieces[4 * step : 4 * step + 4], part, taps, detected)
+        bands.append(band)
+
+    band = jnp.sum(sum(bands), axis=1)[:, :64]
     total = band[:2] + hop(band[2:], 0, 0, 1)
     turned = turn(detected)
     total, turned = lax.optimization_barrier((total, turned))
     other = hop(turned[2:], 0, 0, 1)
     total = total + lax.ppermute(total, "chan", [(i, i ^ 1) for i in range(8)])
+    total = total + lax.ppermute(total, "chan", [(i, i ^ 2) for i in range(8)])
     total, other = lax.optimization_barrier((total, other))
-    total = total + lax.ppermute(total, "chan", [(i, i ^ 2) for i in range(8)])
     total = total + lax.ppermute(total, "chan", [(i, (6 - i // 2 * 2) + i % 2) for i in range(8)])
 
     own = turned[:2]

time: 76.8 us -> 71.9 us (0.936)
  the two profiles are of different devices: /device:TPU:2 before, /device:TPU:24 now
where the time goes in v2:
time: 71.9 us; the launch traced here: 71.4 us
  starting transfers between devices  27.5 us (38%)
  Pallas kernels  19.3 us (27%)
  waiting for transfers between devices  17 us (24%)
  local copies, waits for them, and re-layouts  4.06 us (6%)
  other arithmetic  2.17 us (3%)
  matrix products  1.3 us (2%)
    pallas_call x4, Pallas kernels, detect(): pl.pallas_call(functools.partial(detect_kernel, n // NC), in_specs=in_spe...  11 us
    ppermute x9, starting transfers between devices, hop(): return lax.ppermute(value, 'dm', pairs)  10.4 us
    all_to_all x1, starting transfers between devices, body(): arrived = lax.all_to_all(sent, 'dm', 0, 0, tiled=True)  8.7 us
    pallas_call x2, Pallas kernels, build_taps(): pl.pallas_call(tap_kernel, in_specs=[in_smem(), in_vmem()], out_specs=in_...  7.33 us
    all_to_all x1, waiting for transfers between devices, body(): arrived = lax.all_to_all(sent, 'dm', 0, 0, tiled=True)  6.49 us
    ppermute x9, waiting for transfers between devices, hop(): return lax.ppermute(value, 'dm', pairs)  6.27 us
    ppermute x1, starting transfers between devices, body(): lax.ppermute(total, 'chan', [(i, 6 - i // 2 * 2 + i % 2) for i in range(8)])  5.05 us
    ppermute x1, starting transfers between devices, body(): total = total + lax.ppermute(total, 'chan', [(i, i ^ 2) for i in range(8)])  3.28 us
  transfers between devices with their start and end apart: 13, of which 7 were waited for; matrix products, arithmetic and copies ran while one was open for 5% of the time, Pallas kernels for 23%

profile of v2, /device:TPU:24, one launch (start us, length us, event | category | flops | bytes accessed | tf_op | source)
XLA Modules:
  0.0 71.4 jit_solution(12201240131283261836)
XLA Ops:
  0.0 0.0 copy-start
  0.0 1.0 %copy-done = bf16[1,256,2,512]{3,2,1,0:T(2,128)(2,1)S(1)} copy-done((bf16[1,256,2,512]{3,2,1,0:T(2,128)(2,1)S(1)}, bf16[1,256,2,512]{3,2,1,0:T(2,128)(2,1)}, u32[]{:S(2)}) %copy-start) | copy-done | bytes 524312
  1.0 1.3 %fusion = bf16[512,512]{0,1:T(8,128)(2,1)S(1)} fusion(bf16[256,2,512]{2,1,0:T(2,128)(2,1)S(1)} %bitcast.19, s32[512]{0:T(512)} %constant.48.clone, s32[256]{0:T(256)S(1)} %iota_multiply_fusion), kind=kOutput, calls=%fused_computation.1 | convolution fusion | flops 269221888 | bytes 1051648 | tf_op jit(solution)/shard_map/trc,trk->ck/dot_general | solution.py:255
  2.3 0.8 %copy.11 = bf16[2,16,16,512]{3,2,0,1:T(8,128)(2,1)} copy(bf16[2,16,16,512]{3,2,1,0:T(8,128)(2,1)S(1)} %bitcast.20) | data formatting | bytes 1048576 | tf_op jit(solution)/shard_map/reshape | solution.py:256
  3.2 8.7 %all-to-all-start = ((bf16[32,16,512]{2,1,0:T(8,128)(2,1)}), bf16[32,16,512]{2,1,0:T(8,128)(2,1)S(1)}, u32[]{:S(2)}, u32[]{:S(2)}) async-start(bf16[32,16,512]{2,1,0:T(8,128)(2,1)} %bitcast.6), calls=%async_computation | async-start | bytes 1048576 | tf_op jit(solution)/shard_map/all_to_all | solution.py:257
  11.9 1.3 %constant_dynamic-slice_fusion = (bf16[2,256,512]{2,1,0:T(8,128)(2,1)S(1)}, bf16[2,256,512]{2,1,0:T(8,128)(2,1)S(1)}) fusion(bf16[2,512,512]{2,1,0:T(8,128)(2,1)} %param.7, s32[]{:T(128)S(6)} %select_n.41, s32[]{:T(128)S(6)} %select_n.39), kind=kLoop, calls=%fused_computation.17 | loop fusion | bytes 2097160 | tf_op jit(solution)/shard_map/dynamic_slice | solution.py:249
  13.2 1.6 %collective-permute-start.3 = (bf16[2,256,512]{2,1,0:T(8,128)(2,1)S(1)}, bf16[2,256,512]{2,1,0:T(8,128)(2,1)S(1)}, u32[]{:S(2)}, u32[]{:S(2)}) collective-permute-start(bf16[2,256,512]{2,1,0:T(8,128)(2,1)S(1)} %get-tuple-element.41), channel_id=1, source_target_pairs={{0,8},{8,0},{16,24},{24,16},{32,40},{40,32},{48,56},{56,48},{64,72... | collective-permute-start | bytes 1572872 | tf_op jit(solution)/shard_map/ppermute | solution.py:35
  14.8 0.7 constant_dynamic-slice_fusion.2
  15.4 0.7 broadcast_multiply_fusion
  16.1 0.1 fusion.4
  16.2 0.7 broadcast_clamp_fusion.own_ref
  16.8 6.5 %all-to-all-done.x_ref = bf16[32,16,512]{2,1,0:T(8,128)(2,1)S(1)} async-done(((bf16[32,16,512]{2,1,0:T(8,128)(2,1)}), bf16[32,16,512]{2,1,0:T(8,128)(2,1)S(1)}, u32[]{:S(2)}, u32[]{:S(2)}) %all-to-all-start) | async-done | bytes 524320 | tf_op jit(solution)/shard_map/all_to_all | solution.py:257
  23.3 0.8 %assemble.1 = bf16[16,16,128]{2,1,0:T(8,128)(2,1)S(1)} custom-call(s32[4]{0:T(128)S(1)} %broadcast_clamp_fusion.own_ref, bf16[32,16,512]{2,1,0:T(8,128)(2,1)S(1)} %all-to-all-done.x_ref), custom_call_target="tpu_custom_call" | custom-call | tf_op jit(solution)/shard_map/assemble/pallas_call | solution.py:137
  24.1 0.7 collective-permute-start
  24.8 2.7 %collective-permute-start.1 = (bf16[16,16,128]{2,1,0:T(8,128)(2,1)S(1)}, bf16[16,16,128]{2,1,0:T(8,128)(2,1)S(1)}, u32[]{:S(2)}, u32[]{:S(2)}) collective-permute-start(bf16[16,16,128]{2,1,0:T(8,128)(2,1)S(1)} %assemble.1), channel_id=1, source_target_pairs={{0,48},{8,56},{16,0},{24,8},{32,16},{40,24},{48,32},{56,40},{64,11... | collective-permute-start | bytes 196616 | tf_op jit(solution)/shard_map/ppermute | solution.py:35
  27.5 0.0 collective-permute-start.2
  27.5 3.7 %build_taps.2.t0_ref = bf16[256,64,384]{2,1,0:T(8,128)(2,1)S(1)} custom-call(s32[2]{0:T(128)S(1)} %get-tuple-element.50.live_ref, bf16[2,256,512]{2,1,0:T(8,128)(2,1)S(1)} %get-tuple-element.23.f_ref), custom_call_target="tpu_custom_call" | custom-call | flops 10000000 | bytes 14000000 | tf_op jit(solution)/shard_map/build_taps/pallas_call | solution.py:103
  31.1 0.0 collective-permute-done
  31.2 0.0 collective-permute-done.1
  31.2 2.1 %collective-permute-done.2 = bf16[16,16,128]{2,1,0:T(8,128)(2,1)S(1)} collective-permute-done((bf16[16,16,128]{2,1,0:T(8,128)(2,1)S(1)}, bf16[16,16,128]{2,1,0:T(8,128)(2,1)S(1)}, u32[]{:S(2)}, u32[]{:S(2)}) %collective-permute-start.2) | collective-permute-done | bytes 65568 | tf_op jit(solution)/shard_map/ppermute | solution.py:35
  33.3 2.5 %collective-permute-start.4 = (bf16[64,16,128]{2,1,0:T(8,128)(2,1)S(1)}, bf16[64,16,128]{2,1,0:T(8,128)(2,1)S(1)}, u32[]{:S(2)}, u32[]{:S(2)}) collective-permute-start(bf16[64,16,128]{2,1,0:T(8,128)(2,1)S(1)} %constant_dynamic-update-slice_fusion.x_ref), channel_id=1, source_target_pairs={{0,64},{8,72},{16,80},{24,88},{32,96},{40,104},{48,112},{56,120},{... | collective-permute-start | bytes 786440 | tf_op jit(solution)/shard_map/ppermute | solution.py:35
  35.8 0.0 collective-permute-start.5
  35.8 0.1 slice_bitcast_fusion.3
  35.9 0.0 collective-permute-done.3.f_ref
  35.9 3.7 %build_taps.3.t1_ref = bf16[256,64,384]{2,1,0:T(8,128)(2,1)S(1)} custom-call(s32[2]{0:T(128)S(1)} %get-tuple-element.49.live_ref, bf16[2,256,512]{2,1,0:T(8,128)(2,1)S(1)} %collective-permute-done.3.f_ref), custom_call_target="tpu_custom_call" | custom-call | flops 10000000 | bytes 14000000 | tf_op jit(solution)/shard_map/build_taps/pallas_call | solution.py:103
  39.5 1.8 %collective-permute-start.6 = (bf16[64,16,128]{2,1,0:T(8,128)(2,1)S(1)}, bf16[64,16,128]{2,1,0:T(8,128)(2,1)S(1)}, u32[]{:S(2)}, u32[]{:S(2)}) collective-permute-start(bf16[64,16,128]{2,1,0:T(8,128)(2,1)S(1)} %constant_dynamic-update-slice_fusion.x_ref), channel_id=1, source_target_pairs={{0,128},{8,136},{16,144},{24,152},{32,160},{40,168},{48,176},{56,1... | collective-permute-start | bytes 786440 | tf_op jit(solution)/shard_map/ppermute | solution.py:35
  41.4 2.7 %detect.4 = (f32[4,256,128]{2,1,0:T(8,128)S(1)}, f32[4,8,128]{2,1,0:T(8,128)S(1)}) custom-call(s32[4]{0:T(128)S(1)} %get-tuple-element.45.piece_ref, bf16[256,64,384]{2,1,0:T(8,128)(2,1)S(1)} %build_taps.2.t0_ref, bf16[256,64,384]{2,1,0:T(8,128)(2,1)S(1)} %build_taps.3.t1_ref, bf16[64,16,128]{2,1,0:T(8,128)(2,1)S(1)} %constant_dynamic-update-slice_fusion.x_ref), custom_call_target="tpu_custom_call" | custom-call | flops 1073741824 | bytes 6291456 | tf_op jit(solution)/shard_map/detect/pallas_call | solution.py:207
  44.1 0.0 collective-permute-done.4.x_ref
  44.1 2.8 %detect.5 = (f32[4,256,128]{2,1,0:T(8,128)S(1)}, f32[4,8,128]{2,1,0:T(8,128)S(1)}) custom-call(s32[4]{0:T(128)S(1)} %get-tuple-element.48.piece_ref, bf16[256,64,384]{2,1,0:T(8,128)(2,1)S(1)} %build_taps.2.t0_ref, bf16[256,64,384]{2,1,0:T(8,128)(2,1)S(1)} %build_taps.3.t1_ref, ...), custom_call_target="tpu_custom_call", output_to_operand_aliasing={{0}: (4, {})} | custom-call | flops 1073741824 | bytes 6291456 | tf_op jit(solution)/shard_map/detect/pallas_call | solution.py:207
  46.9 1.3 %collective-permute-done.5.x_ref = bf16[64,16,128]{2,1,0:T(8,128)(2,1)S(1)} collective-permute-done((bf16[64,16,128]{2,1,0:T(8,128)(2,1)S(1)}, bf16[64,16,128]{2,1,0:T(8,128)(2,1)S(1)}, u32[]{:S(2)}, u32[]{:S(2)}) %collective-permute-start.5) | collective-permute-done | bytes 262176 | tf_op jit(solution)/shard_map/ppermute | solution.py:35
  48.2 2.7 %detect.6 = (f32[4,256,128]{2,1,0:T(8,128)S(1)}, f32[4,8,128]{2,1,0:T(8,128)S(1)}) custom-call(s32[4]{0:T(128)S(1)} %get-tuple-element.47.piece_ref, bf16[256,64,384]{2,1,0:T(8,128)(2,1)S(1)} %build_taps.2.t0_ref, bf16[256,64,384]{2,1,0:T(8,128)(2,1)S(1)} %build_taps.3.t1_ref, ...), custom_call_target="tpu_custom_call", output_to_operand_aliasing={{0}: (4, {})} | custom-call | flops 1073741824 | bytes 6291456 | tf_op jit(solution)/shard_map/detect/pallas_call | solution.py:207
  51.0 0.0 collective-permute-done.6.x_ref
  51.0 2.8 %detect.7 = (f32[4,256,128]{2,1,0:T(8,128)S(1)}, f32[4,8,128]{2,1,0:T(8,128)S(1)}) custom-call(s32[4]{0:T(128)S(1)} %get-tuple-element.46.piece_ref, bf16[256,64,384]{2,1,0:T(8,128)(2,1)S(1)} %build_taps.2.t0_ref, bf16[256,64,384]{2,1,0:T(8,128)(2,1)S(1)} %build_taps.3.t1_ref, ...), custom_call_target="tpu_custom_call", output_to_operand_aliasing={{0}: (4, {})} | custom-call | flops 1073741824 | bytes 6291456 | tf_op jit(solution)/shard_map/detect/pallas_call | solution.py:207
  53.7 0.6 collective-permute-start.7
  54.4 0.2 turn.1
  54.5 2.9 %collective-permute-done.7 = f32[2,64]{1,0:T(2,128)S(1)} collective-permute-done((f32[2,64]{1,0:T(2,128)S(1)}, f32[2,64]{1,0:T(2,128)S(1)}, u32[]{:S(2)}, u32[]{:S(2)}) %collective-permute-start.7) | collective-permute-done | bytes 544 | tf_op jit(solution)/shard_map/ppermute | solution.py:35
  57.4 0.6 collective-permute-start.10
  58.0 0.0 collective-permute-start.8
  58.0 1.1 %collective-permute-done.8 = f32[2,64]{1,0:T(2,128)S(1)} collective-permute-done((f32[2,64]{1,0:T(2,128)S(1)}, f32[2,64]{1,0:T(2,128)S(1)}, u32[]{:S(2)}, u32[]{:S(2)}) %collective-permute-start.8) | collective-permute-done | bytes 544 | tf_op jit(solution)/shard_map/ppermute | solution.py:278
  59.2 3.3 %collective-permute-start.9 = (f32[2,64]{1,0:T(2,128)S(1)}, f32[2,64]{1,0:T(2,128)S(1)}, u32[]{:S(2)}, u32[]{:S(2)}) collective-permute-start(f32[2,64]{1,0:T(2,128)S(1)} %add.66), channel_id=1, source_target_pairs={{0,2},{1,3},{2,0},{3,1},{4,6},{5,7},{6,4},{7,5},{8,10},{9,11},{10,... | collective-permute-start | bytes 1544 | tf_op jit(solution)/shard_map/ppermute | solution.py:279
  62.5 1.5 %collective-permute-done.9 = f32[2,64]{1,0:T(2,128)S(1)} collective-permute-done((f32[2,64]{1,0:T(2,128)S(1)}, f32[2,64]{1,0:T(2,128)S(1)}, u32[]{:S(2)}, u32[]{:S(2)}) %collective-permute-start.9) | collective-permute-done | bytes 544 | tf_op jit(solution)/shard_map/ppermute | solution.py:279
  64.0 0.0 collective-permute-done.10
  64.0 5.1 %collective-permute-start.11 = (f32[2,64]{1,0:T(2,128)S(1)}, f32[2,64]{1,0:T(2,128)S(1)}, u32[]{:S(2)}, u32[]{:S(2)}) collective-permute-start(f32[2,64]{1,0:T(2,128)S(1)} %add.67), channel_id=1, source_target_pairs={{0,6},{1,7},{2,4},{3,5},{4,2},{5,3},{6,0},{7,1},{8,14},{9,15},{10,... | collective-permute-start | bytes 1544 | tf_op jit(solution)/shard_map/ppermute | solution.py:281
  69.1 1.5 %collective-permute-done.11 = f32[2,64]{1,0:T(2,128)S(1)} collective-permute-done((f32[2,64]{1,0:T(2,128)S(1)}, f32[2,64]{1,0:T(2,128)S(1)}, u32[]{:S(2)}, u32[]{:S(2)}) %collective-permute-start.11) | collective-permute-done | bytes 544 | tf_op jit(solution)/shard_map/ppermute | solution.py:281
  70.6 0.8 %maximum_divide_fusion = f32[2,64,512]{2,1,0:T(8,128)} fusion(f32[2,64,256]{2,1,0:T(8,128)S(1)} %get-tuple-element.44, f32[2,64,256]{2,1,0:T(8,128)S(1)} %get-tuple-element.43, f32[2,64]{1,0:T(2,128)S(1)} %multiply_add_fusion), kind=kLoop, calls=%fused_computation.6 | loop fusion | flops 131072 | bytes 524800 | tf_op jit(solution)/shard_map/div | solution.py:287
  (13 shorter events, 0.1 us)
Async XLA Ops:
  0.0 1.0 %copy-start = (bf16[1,256,2,512]{3,2,1,0:T(2,128)(2,1)S(1)}, bf16[1,256,2,512]{3,2,1,0:T(2,128)(2,1)}, u32[]{:S(2)}) copy-start(bf16[1,256,2,512]{3,2,1,0:T(2,128)(2,1)} %param.6) | copy-start | bytes 1572868
  3.2 20.2 %all-to-all-start = ((bf16[32,16,512]{2,1,0:T(8,128)(2,1)}), bf16[32,16,512]{2,1,0:T(8,128)(2,1)S(1)}, u32[]{:S(2)}, u32[]{:S(2)}) async-start(bf16[32,16,512]{2,1,0:T(8,128)(2,1)} %bitcast.6), calls=%async_computation | async-start | bytes 1048576 | tf_op jit(solution)/shard_map/all_to_all | solution.py:257
  13.2 22.7 %collective-permute-start.3 = (bf16[2,256,512]{2,1,0:T(8,128)(2,1)S(1)}, bf16[2,256,512]{2,1,0:T(8,128)(2,1)S(1)}, u32[]{:S(2)}, u32[]{:S(2)}) collective-permute-start(bf16[2,256,512]{2,1,0:T(8,128)(2,1)S(1)} %get-tuple-element.41), channel_id=1, source_target_pairs={{0,8},{8,0},{16,24},{24,16},{32,40},{40,32},{48,56},{56,48},{64,72... | collective-permute-start | bytes 1572872 | tf_op jit(solution)/shard_map/ppermute | solution.py:35
  24.1 7.0 %collective-permute-start = (bf16[16,16,128]{2,1,0:T(8,128)(2,1)S(1)}, bf16[16,16,128]{2,1,0:T(8,128)(2,1)S(1)}, u32[]{:S(2)}, u32[]{:S(2)}) collective-permute-start(bf16[16,16,128]{2,1,0:T(8,128)(2,1)S(1)} %assemble.1), channel_id=1, source_target_pairs={{0,16},{8,24},{16,32},{24,40},{32,48},{40,56},{48,0},{56,8},{64,80... | collective-permute-start | bytes 196616 | tf_op jit(solution)/shard_map/ppermute | solution.py:35
  24.8 6.4 %collective-permute-start.1 = (bf16[16,16,128]{2,1,0:T(8,128)(2,1)S(1)}, bf16[16,16,128]{2,1,0:T(8,128)(2,1)S(1)}, u32[]{:S(2)}, u32[]{:S(2)}) collective-permute-start(bf16[16,16,128]{2,1,0:T(8,128)(2,1)S(1)} %assemble.1), channel_id=1, source_target_pairs={{0,48},{8,56},{16,0},{24,8},{32,16},{40,24},{48,32},{56,40},{64,11... | collective-permute-start | bytes 196616 | tf_op jit(solution)/shard_map/ppermute | solution.py:35
  27.5 5.8 %collective-permute-start.2 = (bf16[16,16,128]{2,1,0:T(8,128)(2,1)S(1)}, bf16[16,16,128]{2,1,0:T(8,128)(2,1)S(1)}, u32[]{:S(2)}, u32[]{:S(2)}) collective-permute-start(bf16[16,16,128]{2,1,0:T(8,128)(2,1)S(1)} %assemble.1), channel_id=1, source_target_pairs={{0,32},{8,40},{16,48},{24,56},{32,0},{40,8},{48,16},{56,24},{64,96... | collective-permute-start | bytes 196616 | tf_op jit(solution)/shard_map/ppermute | solution.py:35
  33.3 10.8 %collective-permute-start.4 = (bf16[64,16,128]{2,1,0:T(8,128)(2,1)S(1)}, bf16[64,16,128]{2,1,0:T(8,128)(2,1)S(1)}, u32[]{:S(2)}, u32[]{:S(2)}) collective-permute-start(bf16[64,16,128]{2,1,0:T(8,128)(2,1)S(1)} %constant_dynamic-update-slice_fusion.x_ref), channel_id=1, source_target_pairs={{0,64},{8,72},{16,80},{24,88},{32,96},{40,104},{48,112},{56,120},{... | collective-permute-start | bytes 786440 | tf_op jit(solution)/shard_map/ppermute | solution.py:35
  35.8 12.4 %collective-permute-start.5 = (bf16[64,16,128]{2,1,0:T(8,128)(2,1)S(1)}, bf16[64,16,128]{2,1,0:T(8,128)(2,1)S(1)}, u32[]{:S(2)}, u32[]{:S(2)}) collective-permute-start(bf16[64,16,128]{2,1,0:T(8,128)(2,1)S(1)} %constant_dynamic-update-slice_fusion.x_ref), channel_id=1, source_target_pairs={{0,192},{8,200},{16,208},{24,216},{32,224},{40,232},{48,240},{56,2... | collective-permute-start | bytes 786440 | tf_op jit(solution)/shard_map/ppermute | solution.py:35
  39.5 11.4 %collective-permute-start.6 = (bf16[64,16,128]{2,1,0:T(8,128)(2,1)S(1)}, bf16[64,16,128]{2,1,0:T(8,128)(2,1)S(1)}, u32[]{:S(2)}, u32[]{:S(2)}) collective-permute-start(bf16[64,16,128]{2,1,0:T(8,128)(2,1)S(1)} %constant_dynamic-update-slice_fusion.x_ref), channel_id=1, source_target_pairs={{0,128},{8,136},{16,144},{24,152},{32,160},{40,168},{48,176},{56,1... | collective-permute-start | bytes 786440 | tf_op jit(solution)/shard_map/ppermute | solution.py:35
  53.7 3.7 %collective-permute-start.7 = (f32[2,64]{1,0:T(2,128)S(1)}, f32[2,64]{1,0:T(2,128)S(1)}, u32[]{:S(2)}, u32[]{:S(2)}) collective-permute-start(f32[2,64]{1,0:T(2,128)S(1)} %slice.48), channel_id=1, source_target_pairs={{0,8},{8,0},{16,24},{24,16},{32,40},{40,32},{48,56},{56,48},{64,72... | collective-permute-start | bytes 1544 | tf_op jit(solution)/shard_map/ppermute | solution.py:35
  57.4 6.6 %collective-permute-start.10 = (f32[2,64,256]{2,1,0:T(8,128)S(1)}, f32[2,64,256]{2,1,0:T(8,128)S(1)}, u32[]{:S(2)}, u32[]{:S(2)}) collective-permute-start(f32[2,64,256]{2,1,0:T(8,128)S(1)} %slice.50), channel_id=1, source_target_pairs={{0,8},{8,0},{16,24},{24,16},{32,40},{40,32},{48,56},{56,48},{64,72... | collective-permute-start | bytes 393224 | tf_op jit(solution)/shard_map/ppermute | solution.py:35
  58.0 1.1 %collective-permute-start.8 = (f32[2,64]{1,0:T(2,128)S(1)}, f32[2,64]{1,0:T(2,128)S(1)}, u32[]{:S(2)}, u32[]{:S(2)}) collective-permute-start(f32[2,64]{1,0:T(2,128)S(1)} %slice_add_fusion), channel_id=1, source_target_pairs={{0,1},{1,0},{2,3},{3,2},{4,5},{5,4},{6,7},{7,6},{8,9},{9,8},{10,11... | collective-permute-start | bytes 1544 | tf_op jit(solution)/shard_map/ppermute | solution.py:278
  59.2 4.8 %collective-permute-start.9 = (f32[2,64]{1,0:T(2,128)S(1)}, f32[2,64]{1,0:T(2,128)S(1)}, u32[]{:S(2)}, u32[]{:S(2)}) collective-permute-start(f32[2,64]{1,0:T(2,128)S(1)} %add.66), channel_id=1, source_target_pairs={{0,2},{1,3},{2,0},{3,1},{4,6},{5,7},{6,4},{7,5},{8,10},{9,11},{10,... | collective-permute-start | bytes 1544 | tf_op jit(solution)/shard_map/ppermute | solution.py:279
  64.0 6.6 %collective-permute-start.11 = (f32[2,64]{1,0:T(2,128)S(1)}, f32[2,64]{1,0:T(2,128)S(1)}, u32[]{:S(2)}, u32[]{:S(2)}) collective-permute-start(f32[2,64]{1,0:T(2,128)S(1)} %add.67), channel_id=1, source_target_pairs={{0,6},{1,7},{2,4},{3,5},{4,2},{5,3},{6,0},{7,1},{8,14},{9,15},{10,... | collective-permute-start | bytes 1544 | tf_op jit(solution)/shard_map/ppermute | solution.py:281

commit v3 on v2

--- a/solution.py
+++ b/solution.py
@@ -52,7 +52,7 @@
         y, x, _ = place(i)
         row = []
         for dy in (0, -1, 1, 2):
-            for dx in (0, -1, 1, 2):
+            for dx in (0, 2, -1, 1):
                 row.append(4 * ((y + dy) % 4) + (x + dx) % 4)
         rows.append(row)
     return np.array(rows, np.int32)
@@ -258,7 +258,7 @@
 
     near = assemble(jnp.clip(stretch_owner, 0, DM - 1), arrived)
     stay, near = lax.optimization_barrier((stay, near))
-    line = [hop(near, 0, k, 0) for k in (1, -1, 2)]
+    line = [hop(near, 0, k, 0) for k in (2, 1, -1)]
     taps0 = build_taps(mine, stay)
     taps0, line = lax.optimization_barrier((taps0, line))
     taps = (taps0, build_taps(partner, partner_taps))

time: 71.9 us -> 70.9 us (0.986)
  waiting for transfers between devices: 17 us -> 14.6 us
  starting transfers between devices: 27.5 us -> 28.9 us
    ppermute x9, waiting for transfers between devices: 6.27 us -> 3.93 us  [hop(): return lax.ppermute(value, 'dm', pairs)]
    ppermute x9, starting transfers between devices: 10.4 us -> 11.9 us  [hop(): return lax.ppermute(value, 'dm', pairs)]
  transfers between devices with their start and end apart: 13 -> 13, of which waited for: 7 -> 6; matrix products, arithmetic and copies ran while one was open for 5% -> 5% of each run, Pallas kernels for 23% -> 23%
where the time goes in v3:
time: 70.9 us; the launch traced here: 70.6 us
  starting transfers between devices  28.9 us (41%)
  Pallas kernels  19.3 us (27%)
  waiting for transfers between devices  14.6 us (21%)
  local copies, waits for them, and re-layouts  4.06 us (6%)
  other arithmetic  2.17 us (3%)
  matrix products  1.3 us (2%)
    ppermute x9, starting transfers between devices, hop(): return lax.ppermute(value, 'dm', pairs)  11.9 us
    pallas_call x4, Pallas kernels, detect(): pl.pallas_call(functools.partial(detect_kernel, n // NC), in_specs=in_spe...  11 us
    all_to_all x1, starting transfers between devices, body(): arrived = lax.all_to_all(sent, 'dm', 0, 0, tiled=True)  8.7 us
    pallas_call x2, Pallas kernels, build_taps(): pl.pallas_call(tap_kernel, in_specs=[in_smem(), in_vmem()], out_specs=in_...  7.33 us
    all_to_all x1, waiting for transfers between devices, body(): arrived = lax.all_to_all(sent, 'dm', 0, 0, tiled=True)  6.49 us
    ppermute x1, starting transfers between devices, body(): lax.ppermute(total, 'chan', [(i, 6 - i // 2 * 2 + i % 2) for i in range(8)])  5.05 us
    ppermute x9, waiting for transfers between devices, hop(): return lax.ppermute(value, 'dm', pairs)  3.93 us
    ppermute x1, starting transfers between devices, body(): total = total + lax.ppermute(total, 'chan', [(i, i ^ 2) for i in range(8)])  3.26 us
  transfers between devices with their start and end apart: 13, of which 6 were waited for; matrix products, arithmetic and copies ran while one was open for 5% of the time, Pallas kernels for 23%

profile of v3, /device:TPU:24, one launch (start us, length us, event | category | flops | bytes accessed | tf_op | source)
XLA Modules:
  0.0 70.6 jit_solution(17274423797821963839)
XLA Ops:
  0.0 0.0 copy-start
  0.0 1.0 %copy-done = bf16[1,256,2,512]{3,2,1,0:T(2,128)(2,1)S(1)} copy-done((bf16[1,256,2,512]{3,2,1,0:T(2,128)(2,1)S(1)}, bf16[1,256,2,512]{3,2,1,0:T(2,128)(2,1)}, u32[]{:S(2)}) %copy-start) | copy-done | bytes 524312
  1.0 1.3 %fusion = bf16[512,512]{0,1:T(8,128)(2,1)S(1)} fusion(bf16[256,2,512]{2,1,0:T(2,128)(2,1)S(1)} %bitcast.19, s32[512]{0:T(512)} %constant.48.clone, s32[256]{0:T(256)S(1)} %iota_multiply_fusion), kind=kOutput, calls=%fused_computation.1 | convolution fusion | flops 269221888 | bytes 1051648 | tf_op jit(solution)/shard_map/trc,trk->ck/dot_general | solution.py:255
  2.3 0.8 %copy.11 = bf16[2,16,16,512]{3,2,0,1:T(8,128)(2,1)} copy(bf16[2,16,16,512]{3,2,1,0:T(8,128)(2,1)S(1)} %bitcast.20) | data formatting | bytes 1048576 | tf_op jit(solution)/shard_map/reshape | solution.py:256
  3.2 8.7 %all-to-all-start = ((bf16[32,16,512]{2,1,0:T(8,128)(2,1)}), bf16[32,16,512]{2,1,0:T(8,128)(2,1)S(1)}, u32[]{:S(2)}, u32[]{:S(2)}) async-start(bf16[32,16,512]{2,1,0:T(8,128)(2,1)} %bitcast.6), calls=%async_computation | async-start | bytes 1048576 | tf_op jit(solution)/shard_map/all_to_all | solution.py:257
  11.9 1.3 %constant_dynamic-slice_fusion = (bf16[2,256,512]{2,1,0:T(8,128)(2,1)S(1)}, bf16[2,256,512]{2,1,0:T(8,128)(2,1)S(1)}) fusion(bf16[2,512,512]{2,1,0:T(8,128)(2,1)} %param.7, s32[]{:T(128)S(6)} %select_n.41, s32[]{:T(128)S(6)} %select_n.39), kind=kLoop, calls=%fused_computation.17 | loop fusion | bytes 2097160 | tf_op jit(solution)/shard_map/dynamic_slice | solution.py:249
  13.2 1.6 %collective-permute-start.3 = (bf16[2,256,512]{2,1,0:T(8,128)(2,1)S(1)}, bf16[2,256,512]{2,1,0:T(8,128)(2,1)S(1)}, u32[]{:S(2)}, u32[]{:S(2)}) collective-permute-start(bf16[2,256,512]{2,1,0:T(8,128)(2,1)S(1)} %get-tuple-element.41), channel_id=1, source_target_pairs={{0,8},{8,0},{16,24},{24,16},{32,40},{40,32},{48,56},{56,48},{64,72... | collective-permute-start | bytes 1572872 | tf_op jit(solution)/shard_map/ppermute | solution.py:35
  14.8 0.7 constant_dynamic-slice_fusion.2
  15.4 0.7 broadcast_multiply_fusion
  16.1 0.1 fusion.4
  16.2 0.7 broadcast_clamp_fusion.own_ref
  16.8 6.5 %all-to-all-done.x_ref = bf16[32,16,512]{2,1,0:T(8,128)(2,1)S(1)} async-done(((bf16[32,16,512]{2,1,0:T(8,128)(2,1)}), bf16[32,16,512]{2,1,0:T(8,128)(2,1)S(1)}, u32[]{:S(2)}, u32[]{:S(2)}) %all-to-all-start) | async-done | bytes 524320 | tf_op jit(solution)/shard_map/all_to_all | solution.py:257
  23.3 0.8 %assemble.1 = bf16[16,16,128]{2,1,0:T(8,128)(2,1)S(1)} custom-call(s32[4]{0:T(128)S(1)} %broadcast_clamp_fusion.own_ref, bf16[32,16,512]{2,1,0:T(8,128)(2,1)S(1)} %all-to-all-done.x_ref), custom_call_target="tpu_custom_call" | custom-call | tf_op jit(solution)/shard_map/assemble/pallas_call | solution.py:137
  24.1 1.1 %collective-permute-start = (bf16[16,16,128]{2,1,0:T(8,128)(2,1)S(1)}, bf16[16,16,128]{2,1,0:T(8,128)(2,1)S(1)}, u32[]{:S(2)}, u32[]{:S(2)}) collective-permute-start(bf16[16,16,128]{2,1,0:T(8,128)(2,1)S(1)} %assemble.1), channel_id=1, source_target_pairs={{0,32},{8,40},{16,48},{24,56},{32,0},{40,8},{48,16},{56,24},{64,96... | collective-permute-start | bytes 196616 | tf_op jit(solution)/shard_map/ppermute | solution.py:35
  25.3 0.7 %collective-permute-start.1 = (bf16[16,16,128]{2,1,0:T(8,128)(2,1)S(1)}, bf16[16,16,128]{2,1,0:T(8,128)(2,1)S(1)}, u32[]{:S(2)}, u32[]{:S(2)}) collective-permute-start(bf16[16,16,128]{2,1,0:T(8,128)(2,1)S(1)} %assemble.1), channel_id=1, source_target_pairs={{0,16},{8,24},{16,32},{24,40},{32,48},{40,56},{48,0},{56,8},{64,80... | collective-permute-start | bytes 196616 | tf_op jit(solution)/shard_map/ppermute | solution.py:35
  26.0 2.5 %collective-permute-start.2 = (bf16[16,16,128]{2,1,0:T(8,128)(2,1)S(1)}, bf16[16,16,128]{2,1,0:T(8,128)(2,1)S(1)}, u32[]{:S(2)}, u32[]{:S(2)}) collective-permute-start(bf16[16,16,128]{2,1,0:T(8,128)(2,1)S(1)} %assemble.1), channel_id=1, source_target_pairs={{0,48},{8,56},{16,0},{24,8},{32,16},{40,24},{48,32},{56,40},{64,11... | collective-permute-start | bytes 196616 | tf_op jit(solution)/shard_map/ppermute | solution.py:35
  28.5 3.7 %build_taps.2.t0_ref = bf16[256,64,384]{2,1,0:T(8,128)(2,1)S(1)} custom-call(s32[2]{0:T(128)S(1)} %get-tuple-element.50.live_ref, bf16[2,256,512]{2,1,0:T(8,128)(2,1)S(1)} %get-tuple-element.23.f_ref), custom_call_target="tpu_custom_call" | custom-call | flops 10000000 | bytes 14000000 | tf_op jit(solution)/shard_map/build_taps/pallas_call | solution.py:103
  32.2 0.0 collective-permute-done
  32.2 0.0 collective-permute-done.1
  32.2 0.0 collective-permute-done.2
  32.3 2.2 %collective-permute-start.4 = (bf16[64,16,128]{2,1,0:T(8,128)(2,1)S(1)}, bf16[64,16,128]{2,1,0:T(8,128)(2,1)S(1)}, u32[]{:S(2)}, u32[]{:S(2)}) collective-permute-start(bf16[64,16,128]{2,1,0:T(8,128)(2,1)S(1)} %constant_dynamic-update-slice_fusion.x_ref), channel_id=1, source_target_pairs={{0,64},{8,72},{16,80},{24,88},{32,96},{40,104},{48,112},{56,120},{... | collective-permute-start | bytes 786440 | tf_op jit(solution)/shard_map/ppermute | solution.py:35
  34.5 0.0 collective-permute-start.5
  34.5 0.1 slice_bitcast_fusion.3
  34.6 0.0 collective-permute-done.3.f_ref
  34.6 3.7 %build_taps.3.t1_ref = bf16[256,64,384]{2,1,0:T(8,128)(2,1)S(1)} custom-call(s32[2]{0:T(128)S(1)} %get-tuple-element.49.live_ref, bf16[2,256,512]{2,1,0:T(8,128)(2,1)S(1)} %collective-permute-done.3.f_ref), custom_call_target="tpu_custom_call" | custom-call | flops 10000000 | bytes 14000000 | tf_op jit(solution)/shard_map/build_taps/pallas_call | solution.py:103
  38.2 2.3 %collective-permute-start.6 = (bf16[64,16,128]{2,1,0:T(8,128)(2,1)S(1)}, bf16[64,16,128]{2,1,0:T(8,128)(2,1)S(1)}, u32[]{:S(2)}, u32[]{:S(2)}) collective-permute-start(bf16[64,16,128]{2,1,0:T(8,128)(2,1)S(1)} %constant_dynamic-update-slice_fusion.x_ref), channel_id=1, source_target_pairs={{0,128},{8,136},{16,144},{24,152},{32,160},{40,168},{48,176},{56,1... | collective-permute-start | bytes 786440 | tf_op jit(solution)/shard_map/ppermute | solution.py:35
  40.6 2.7 %detect.4 = (f32[4,256,128]{2,1,0:T(8,128)S(1)}, f32[4,8,128]{2,1,0:T(8,128)S(1)}) custom-call(s32[4]{0:T(128)S(1)} %get-tuple-element.45.piece_ref, bf16[256,64,384]{2,1,0:T(8,128)(2,1)S(1)} %build_taps.2.t0_ref, bf16[256,64,384]{2,1,0:T(8,128)(2,1)S(1)} %build_taps.3.t1_ref, bf16[64,16,128]{2,1,0:T(8,128)(2,1)S(1)} %constant_dynamic-update-slice_fusion.x_ref), custom_call_target="tpu_custom_call" | custom-call | flops 1073741824 | bytes 6291456 | tf_op jit(solution)/shard_map/detect/pallas_call | solution.py:207
  43.3 0.0 collective-permute-done.4.x_ref
  43.3 2.8 %detect.5 = (f32[4,256,128]{2,1,0:T(8,128)S(1)}, f32[4,8,128]{2,1,0:T(8,128)S(1)}) custom-call(s32[4]{0:T(128)S(1)} %get-tuple-element.48.piece_ref, bf16[256,64,384]{2,1,0:T(8,128)(2,1)S(1)} %build_taps.2.t0_ref, bf16[256,64,384]{2,1,0:T(8,128)(2,1)S(1)} %build_taps.3.t1_ref, ...), custom_call_target="tpu_custom_call", output_to_operand_aliasing={{0}: (4, {})} | custom-call | flops 1073741824 | bytes 6291456 | tf_op jit(solution)/shard_map/detect/pallas_call | solution.py:207
  46.1 1.2 %collective-permute-done.5.x_ref = bf16[64,16,128]{2,1,0:T(8,128)(2,1)S(1)} collective-permute-done((bf16[64,16,128]{2,1,0:T(8,128)(2,1)S(1)}, bf16[64,16,128]{2,1,0:T(8,128)(2,1)S(1)}, u32[]{:S(2)}, u32[]{:S(2)}) %collective-permute-start.5) | collective-permute-done | bytes 262176 | tf_op jit(solution)/shard_map/ppermute | solution.py:35
  47.3 2.7 %detect.6 = (f32[4,256,128]{2,1,0:T(8,128)S(1)}, f32[4,8,128]{2,1,0:T(8,128)S(1)}) custom-call(s32[4]{0:T(128)S(1)} %get-tuple-element.47.piece_ref, bf16[256,64,384]{2,1,0:T(8,128)(2,1)S(1)} %build_taps.2.t0_ref, bf16[256,64,384]{2,1,0:T(8,128)(2,1)S(1)} %build_taps.3.t1_ref, ...), custom_call_target="tpu_custom_call", output_to_operand_aliasing={{0}: (4, {})} | custom-call | flops 1073741824 | bytes 6291456 | tf_op jit(solution)/shard_map/detect/pallas_call | solution.py:207
  50.0 0.0 collective-permute-done.6.x_ref
  50.0 2.8 %detect.7 = (f32[4,256,128]{2,1,0:T(8,128)S(1)}, f32[4,8,128]{2,1,0:T(8,128)S(1)}) custom-call(s32[4]{0:T(128)S(1)} %get-tuple-element.46.piece_ref, bf16[256,64,384]{2,1,0:T(8,128)(2,1)S(1)} %build_taps.2.t0_ref, bf16[256,64,384]{2,1,0:T(8,128)(2,1)S(1)} %build_taps.3.t1_ref, ...), custom_call_target="tpu_custom_call", output_to_operand_aliasing={{0}: (4, {})} | custom-call | flops 1073741824 | bytes 6291456 | tf_op jit(solution)/shard_map/detect/pallas_call | solution.py:207
  52.8 0.7 %collective-permute-start.7 = (f32[2,64]{1,0:T(2,128)S(1)}, f32[2,64]{1,0:T(2,128)S(1)}, u32[]{:S(2)}, u32[]{:S(2)}) collective-permute-start(f32[2,64]{1,0:T(2,128)S(1)} %slice.48), channel_id=1, source_target_pairs={{0,8},{8,0},{16,24},{24,16},{32,40},{40,32},{48,56},{56,48},{64,72... | collective-permute-start | bytes 1544 | tf_op jit(solution)/shard_map/ppermute | solution.py:35
  53.5 0.2 turn.1
  53.7 2.7 %collective-permute-done.7 = f32[2,64]{1,0:T(2,128)S(1)} collective-permute-done((f32[2,64]{1,0:T(2,128)S(1)}, f32[2,64]{1,0:T(2,128)S(1)}, u32[]{:S(2)}, u32[]{:S(2)}) %collective-permute-start.7) | collective-permute-done | bytes 544 | tf_op jit(solution)/shard_map/ppermute | solution.py:35
  56.5 0.7 %collective-permute-start.10 = (f32[2,64,256]{2,1,0:T(8,128)S(1)}, f32[2,64,256]{2,1,0:T(8,128)S(1)}, u32[]{:S(2)}, u32[]{:S(2)}) collective-permute-start(f32[2,64,256]{2,1,0:T(8,128)S(1)} %slice.50), channel_id=1, source_target_pairs={{0,8},{8,0},{16,24},{24,16},{32,40},{40,32},{48,56},{56,48},{64,72... | collective-permute-start | bytes 393224 | tf_op jit(solution)/shard_map/ppermute | solution.py:35
  57.2 0.0 collective-permute-start.8
  57.2 1.1 %collective-permute-done.8 = f32[2,64]{1,0:T(2,128)S(1)} collective-permute-done((f32[2,64]{1,0:T(2,128)S(1)}, f32[2,64]{1,0:T(2,128)S(1)}, u32[]{:S(2)}, u32[]{:S(2)}) %collective-permute-start.8) | collective-permute-done | bytes 544 | tf_op jit(solution)/shard_map/ppermute | solution.py:278
  58.3 3.3 %collective-permute-start.9 = (f32[2,64]{1,0:T(2,128)S(1)}, f32[2,64]{1,0:T(2,128)S(1)}, u32[]{:S(2)}, u32[]{:S(2)}) collective-permute-start(f32[2,64]{1,0:T(2,128)S(1)} %add.66), channel_id=1, source_target_pairs={{0,2},{1,3},{2,0},{3,1},{4,6},{5,7},{6,4},{7,5},{8,10},{9,11},{10,... | collective-permute-start | bytes 1544 | tf_op jit(solution)/shard_map/ppermute | solution.py:279
  61.6 1.5 %collective-permute-done.9 = f32[2,64]{1,0:T(2,128)S(1)} collective-permute-done((f32[2,64]{1,0:T(2,128)S(1)}, f32[2,64]{1,0:T(2,128)S(1)}, u32[]{:S(2)}, u32[]{:S(2)}) %collective-permute-start.9) | collective-permute-done | bytes 544 | tf_op jit(solution)/shard_map/ppermute | solution.py:279
  63.2 0.0 collective-permute-done.10
  63.2 5.1 %collective-permute-start.11 = (f32[2,64]{1,0:T(2,128)S(1)}, f32[2,64]{1,0:T(2,128)S(1)}, u32[]{:S(2)}, u32[]{:S(2)}) collective-permute-start(f32[2,64]{1,0:T(2,128)S(1)} %add.67), channel_id=1, source_target_pairs={{0,6},{1,7},{2,4},{3,5},{4,2},{5,3},{6,0},{7,1},{8,14},{9,15},{10,... | collective-permute-start | bytes 1544 | tf_op jit(solution)/shard_map/ppermute | solution.py:281
  68.2 1.5 %collective-permute-done.11 = f32[2,64]{1,0:T(2,128)S(1)} collective-permute-done((f32[2,64]{1,0:T(2,128)S(1)}, f32[2,64]{1,0:T(2,128)S(1)}, u32[]{:S(2)}, u32[]{:S(2)}) %collective-permute-start.11) | collective-permute-done | bytes 544 | tf_op jit(solution)/shard_map/ppermute | solution.py:281
  69.8 0.8 %maximum_divide_fusion = f32[2,64,512]{2,1,0:T(8,128)} fusion(f32[2,64,256]{2,1,0:T(8,128)S(1)} %get-tuple-element.44, f32[2,64,256]{2,1,0:T(8,128)S(1)} %get-tuple-element.43, f32[2,64]{1,0:T(2,128)S(1)} %multiply_add_fusion), kind=kLoop, calls=%fused_computation.6 | loop fusion | flops 131072 | bytes 524800 | tf_op jit(solution)/shard_map/div | solution.py:287
  (13 shorter events, 0.1 us)
Async XLA Ops:
  0.0 1.0 %copy-start = (bf16[1,256,2,512]{3,2,1,0:T(2,128)(2,1)S(1)}, bf16[1,256,2,512]{3,2,1,0:T(2,128)(2,1)}, u32[]{:S(2)}) copy-start(bf16[1,256,2,512]{3,2,1,0:T(2,128)(2,1)} %param.6) | copy-start | bytes 1572868
  3.2 20.2 %all-to-all-start = ((bf16[32,16,512]{2,1,0:T(8,128)(2,1)}), bf16[32,16,512]{2,1,0:T(8,128)(2,1)S(1)}, u32[]{:S(2)}, u32[]{:S(2)}) async-start(bf16[32,16,512]{2,1,0:T(8,128)(2,1)} %bitcast.6), calls=%async_computation | async-start | bytes 1048576 | tf_op jit(solution)/shard_map/all_to_all | solution.py:257
  13.2 21.4 %collective-permute-start.3 = (bf16[2,256,512]{2,1,0:T(8,128)(2,1)S(1)}, bf16[2,256,512]{2,1,0:T(8,128)(2,1)S(1)}, u32[]{:S(2)}, u32[]{:S(2)}) collective-permute-start(bf16[2,256,512]{2,1,0:T(8,128)(2,1)S(1)} %get-tuple-element.41), channel_id=1, source_target_pairs={{0,8},{8,0},{16,24},{24,16},{32,40},{40,32},{48,56},{56,48},{64,72... | collective-permute-start | bytes 1572872 | tf_op jit(solution)/shard_map/ppermute | solution.py:35
  24.1 8.1 %collective-permute-start = (bf16[16,16,128]{2,1,0:T(8,128)(2,1)S(1)}, bf16[16,16,128]{2,1,0:T(8,128)(2,1)S(1)}, u32[]{:S(2)}, u32[]{:S(2)}) collective-permute-start(bf16[16,16,128]{2,1,0:T(8,128)(2,1)S(1)} %assemble.1), channel_id=1, source_target_pairs={{0,32},{8,40},{16,48},{24,56},{32,0},{40,8},{48,16},{56,24},{64,96... | collective-permute-start | bytes 196616 | tf_op jit(solution)/shard_map/ppermute | solution.py:35
  25.3 6.9 %collective-permute-start.1 = (bf16[16,16,128]{2,1,0:T(8,128)(2,1)S(1)}, bf16[16,16,128]{2,1,0:T(8,128)(2,1)S(1)}, u32[]{:S(2)}, u32[]{:S(2)}) collective-permute-start(bf16[16,16,128]{2,1,0:T(8,128)(2,1)S(1)} %assemble.1), channel_id=1, source_target_pairs={{0,16},{8,24},{16,32},{24,40},{32,48},{40,56},{48,0},{56,8},{64,80... | collective-permute-start | bytes 196616 | tf_op jit(solution)/shard_map/ppermute | solution.py:35
  26.0 6.2 %collective-permute-start.2 = (bf16[16,16,128]{2,1,0:T(8,128)(2,1)S(1)}, bf16[16,16,128]{2,1,0:T(8,128)(2,1)S(1)}, u32[]{:S(2)}, u32[]{:S(2)}) collective-permute-start(bf16[16,16,128]{2,1,0:T(8,128)(2,1)S(1)} %assemble.1), channel_id=1, source_target_pairs={{0,48},{8,56},{16,0},{24,8},{32,16},{40,24},{48,32},{56,40},{64,11... | collective-permute-start | bytes 196616 | tf_op jit(solution)/shard_map/ppermute | solution.py:35
  32.3 11.0 %collective-permute-start.4 = (bf16[64,16,128]{2,1,0:T(8,128)(2,1)S(1)}, bf16[64,16,128]{2,1,0:T(8,128)(2,1)S(1)}, u32[]{:S(2)}, u32[]{:S(2)}) collective-permute-start(bf16[64,16,128]{2,1,0:T(8,128)(2,1)S(1)} %constant_dynamic-update-slice_fusion.x_ref), channel_id=1, source_target_pairs={{0,64},{8,72},{16,80},{24,88},{32,96},{40,104},{48,112},{56,120},{... | collective-permute-start | bytes 786440 | tf_op jit(solution)/shard_map/ppermute | solution.py:35
  34.5 12.8 %collective-permute-start.5 = (bf16[64,16,128]{2,1,0:T(8,128)(2,1)S(1)}, bf16[64,16,128]{2,1,0:T(8,128)(2,1)S(1)}, u32[]{:S(2)}, u32[]{:S(2)}) collective-permute-start(bf16[64,16,128]{2,1,0:T(8,128)(2,1)S(1)} %constant_dynamic-update-slice_fusion.x_ref), channel_id=1, source_target_pairs={{0,192},{8,200},{16,208},{24,216},{32,224},{40,232},{48,240},{56,2... | collective-permute-start | bytes 786440 | tf_op jit(solution)/shard_map/ppermute | solution.py:35
  38.2 11.8 %collective-permute-start.6 = (bf16[64,16,128]{2,1,0:T(8,128)(2,1)S(1)}, bf16[64,16,128]{2,1,0:T(8,128)(2,1)S(1)}, u32[]{:S(2)}, u32[]{:S(2)}) collective-permute-start(bf16[64,16,128]{2,1,0:T(8,128)(2,1)S(1)} %constant_dynamic-update-slice_fusion.x_ref), channel_id=1, source_target_pairs={{0,128},{8,136},{16,144},{24,152},{32,160},{40,168},{48,176},{56,1... | collective-permute-start | bytes 786440 | tf_op jit(solution)/shard_map/ppermute | solution.py:35
  52.8 3.7 %collective-permute-start.7 = (f32[2,64]{1,0:T(2,128)S(1)}, f32[2,64]{1,0:T(2,128)S(1)}, u32[]{:S(2)}, u32[]{:S(2)}) collective-permute-start(f32[2,64]{1,0:T(2,128)S(1)} %slice.48), channel_id=1, source_target_pairs={{0,8},{8,0},{16,24},{24,16},{32,40},{40,32},{48,56},{56,48},{64,72... | collective-permute-start | bytes 1544 | tf_op jit(solution)/shard_map/ppermute | solution.py:35
  56.5 6.7 %collective-permute-start.10 = (f32[2,64,256]{2,1,0:T(8,128)S(1)}, f32[2,64,256]{2,1,0:T(8,128)S(1)}, u32[]{:S(2)}, u32[]{:S(2)}) collective-permute-start(f32[2,64,256]{2,1,0:T(8,128)S(1)} %slice.50), channel_id=1, source_target_pairs={{0,8},{8,0},{16,24},{24,16},{32,40},{40,32},{48,56},{56,48},{64,72... | collective-permute-start | bytes 393224 | tf_op jit(solution)/shard_map/ppermute | solution.py:35
  57.2 1.1 %collective-permute-start.8 = (f32[2,64]{1,0:T(2,128)S(1)}, f32[2,64]{1,0:T(2,128)S(1)}, u32[]{:S(2)}, u32[]{:S(2)}) collective-permute-start(f32[2,64]{1,0:T(2,128)S(1)} %slice_add_fusion), channel_id=1, source_target_pairs={{0,1},{1,0},{2,3},{3,2},{4,5},{5,4},{6,7},{7,6},{8,9},{9,8},{10,11... | collective-permute-start | bytes 1544 | tf_op jit(solution)/shard_map/ppermute | solution.py:278
  58.3 4.8 %collective-permute-start.9 = (f32[2,64]{1,0:T(2,128)S(1)}, f32[2,64]{1,0:T(2,128)S(1)}, u32[]{:S(2)}, u32[]{:S(2)}) collective-permute-start(f32[2,64]{1,0:T(2,128)S(1)} %add.66), channel_id=1, source_target_pairs={{0,2},{1,3},{2,0},{3,1},{4,6},{5,7},{6,4},{7,5},{8,10},{9,11},{10,... | collective-permute-start | bytes 1544 | tf_op jit(solution)/shard_map/ppermute | solution.py:279
  63.2 6.6 %collective-permute-start.11 = (f32[2,64]{1,0:T(2,128)S(1)}, f32[2,64]{1,0:T(2,128)S(1)}, u32[]{:S(2)}, u32[]{:S(2)}) collective-permute-start(f32[2,64]{1,0:T(2,128)S(1)} %add.67), channel_id=1, source_target_pairs={{0,6},{1,7},{2,4},{3,5},{4,2},{5,3},{6,0},{7,1},{8,14},{9,15},{10,... | collective-permute-start | bytes 1544 | tf_op jit(solution)/shard_map/ppermute | solution.py:281

commit v4 on v3

--- a/solution.py
+++ b/solution.py
@@ -58,7 +58,7 @@
     return np.array(rows, np.int32)
 
 
-TAP_CH = 32
+TAP_CH = 64
 
 
 def tap_kernel(live_ref, f_ref, o_ref, scr):

time: 70.9 us -> 70.5 us (level)
  no operation moved by 1% of the time
where the time goes in v4:
time: 70.5 us; the launch traced here: 70.2 us
  starting transfers between devices  28.8 us (41%)
  Pallas kernels  18.8 us (27%)
  waiting for transfers between devices  14.9 us (21%)
  local copies, waits for them, and re-layouts  4.06 us (6%)
  other arithmetic  2.17 us (3%)
  matrix products  1.3 us (2%)
    ppermute x9, starting transfers between devices, hop(): return lax.ppermute(value, 'dm', pairs)  11.8 us
    pallas_call x4, Pallas kernels, detect(): pl.pallas_call(functools.partial(detect_kernel, n // NC), in_specs=in_spe...  11 us
    all_to_all x1, starting transfers between devices, body(): arrived = lax.all_to_all(sent, 'dm', 0, 0, tiled=True)  8.7 us
    pallas_call x2, Pallas kernels, build_taps(): pl.pallas_call(tap_kernel, in_specs=[in_smem(), in_vmem()], out_specs=in_...  6.84 us
    all_to_all x1, waiting for transfers between devices, body(): arrived = lax.all_to_all(sent, 'dm', 0, 0, tiled=True)  6.49 us
    ppermute x1, starting transfers between devices, body(): lax.ppermute(total, 'chan', [(i, 6 - i // 2 * 2 + i % 2) for i in range(8)])  5.05 us
    ppermute x9, waiting for transfers between devices, hop(): return lax.ppermute(value, 'dm', pairs)  4.16 us
    ppermute x1, starting transfers between devices, body(): total = total + lax.ppermute(total, 'chan', [(i, i ^ 2) for i in range(8)])  3.26 us
  transfers between devices with their start and end apart: 13, of which 6 were waited for; matrix products, arithmetic and copies ran while one was open for 5% of the time, Pallas kernels for 23%

profile of v4, /device:TPU:24, one launch (start us, length us, event | category | flops | bytes accessed | tf_op | source)
XLA Modules:
  0.0 70.2 jit_solution(10698477573703875187)
XLA Ops:
  0.0 0.0 copy-start
  0.0 1.0 %copy-done = bf16[1,256,2,512]{3,2,1,0:T(2,128)(2,1)S(1)} copy-done((bf16[1,256,2,512]{3,2,1,0:T(2,128)(2,1)S(1)}, bf16[1,256,2,512]{3,2,1,0:T(2,128)(2,1)}, u32[]{:S(2)}) %copy-start) | copy-done | bytes 524312
  1.0 1.3 %fusion = bf16[512,512]{0,1:T(8,128)(2,1)S(1)} fusion(bf16[256,2,512]{2,1,0:T(2,128)(2,1)S(1)} %bitcast.19, s32[512]{0:T(512)} %constant.48.clone, s32[256]{0:T(256)S(1)} %iota_multiply_fusion), kind=kOutput, calls=%fused_computation.1 | convolution fusion | flops 269221888 | bytes 1051648 | tf_op jit(solution)/shard_map/trc,trk->ck/dot_general | solution.py:255
  2.3 0.8 %copy.11 = bf16[2,16,16,512]{3,2,0,1:T(8,128)(2,1)} copy(bf16[2,16,16,512]{3,2,1,0:T(8,128)(2,1)S(1)} %bitcast.20) | data formatting | bytes 1048576 | tf_op jit(solution)/shard_map/reshape | solution.py:256
  3.2 8.7 %all-to-all-start = ((bf16[32,16,512]{2,1,0:T(8,128)(2,1)}), bf16[32,16,512]{2,1,0:T(8,128)(2,1)S(1)}, u32[]{:S(2)}, u32[]{:S(2)}) async-start(bf16[32,16,512]{2,1,0:T(8,128)(2,1)} %bitcast.6), calls=%async_computation | async-start | bytes 1048576 | tf_op jit(solution)/shard_map/all_to_all | solution.py:257
  11.9 1.3 %constant_dynamic-slice_fusion = (bf16[2,256,512]{2,1,0:T(8,128)(2,1)S(1)}, bf16[2,256,512]{2,1,0:T(8,128)(2,1)S(1)}) fusion(bf16[2,512,512]{2,1,0:T(8,128)(2,1)} %param.7, s32[]{:T(128)S(6)} %select_n.41, s32[]{:T(128)S(6)} %select_n.39), kind=kLoop, calls=%fused_computation.17 | loop fusion | bytes 2097160 | tf_op jit(solution)/shard_map/dynamic_slice | solution.py:249
  13.2 1.6 %collective-permute-start.3 = (bf16[2,256,512]{2,1,0:T(8,128)(2,1)S(1)}, bf16[2,256,512]{2,1,0:T(8,128)(2,1)S(1)}, u32[]{:S(2)}, u32[]{:S(2)}) collective-permute-start(bf16[2,256,512]{2,1,0:T(8,128)(2,1)S(1)} %get-tuple-element.41), channel_id=1, source_target_pairs={{0,8},{8,0},{16,24},{24,16},{32,40},{40,32},{48,56},{56,48},{64,72... | collective-permute-start | bytes 1572872 | tf_op jit(solution)/shard_map/ppermute | solution.py:35
  14.8 0.7 constant_dynamic-slice_fusion.2
  15.4 0.7 broadcast_multiply_fusion
  16.1 0.1 fusion.4
  16.2 0.7 broadcast_clamp_fusion.own_ref
  16.8 6.5 %all-to-all-done.x_ref = bf16[32,16,512]{2,1,0:T(8,128)(2,1)S(1)} async-done(((bf16[32,16,512]{2,1,0:T(8,128)(2,1)}), bf16[32,16,512]{2,1,0:T(8,128)(2,1)S(1)}, u32[]{:S(2)}, u32[]{:S(2)}) %all-to-all-start) | async-done | bytes 524320 | tf_op jit(solution)/shard_map/all_to_all | solution.py:257
  23.3 0.8 %assemble.1 = bf16[16,16,128]{2,1,0:T(8,128)(2,1)S(1)} custom-call(s32[4]{0:T(128)S(1)} %broadcast_clamp_fusion.own_ref, bf16[32,16,512]{2,1,0:T(8,128)(2,1)S(1)} %all-to-all-done.x_ref), custom_call_target="tpu_custom_call" | custom-call | tf_op jit(solution)/shard_map/assemble/pallas_call | solution.py:137
  24.1 1.1 %collective-permute-start = (bf16[16,16,128]{2,1,0:T(8,128)(2,1)S(1)}, bf16[16,16,128]{2,1,0:T(8,128)(2,1)S(1)}, u32[]{:S(2)}, u32[]{:S(2)}) collective-permute-start(bf16[16,16,128]{2,1,0:T(8,128)(2,1)S(1)} %assemble.1), channel_id=1, source_target_pairs={{0,32},{8,40},{16,48},{24,56},{32,0},{40,8},{48,16},{56,24},{64,96... | collective-permute-start | bytes 196616 | tf_op jit(solution)/shard_map/ppermute | solution.py:35
  25.3 0.7 %collective-permute-start.1 = (bf16[16,16,128]{2,1,0:T(8,128)(2,1)S(1)}, bf16[16,16,128]{2,1,0:T(8,128)(2,1)S(1)}, u32[]{:S(2)}, u32[]{:S(2)}) collective-permute-start(bf16[16,16,128]{2,1,0:T(8,128)(2,1)S(1)} %assemble.1), channel_id=1, source_target_pairs={{0,16},{8,24},{16,32},{24,40},{32,48},{40,56},{48,0},{56,8},{64,80... | collective-permute-start | bytes 196616 | tf_op jit(solution)/shard_map/ppermute | solution.py:35
  26.0 2.5 %collective-permute-start.2 = (bf16[16,16,128]{2,1,0:T(8,128)(2,1)S(1)}, bf16[16,16,128]{2,1,0:T(8,128)(2,1)S(1)}, u32[]{:S(2)}, u32[]{:S(2)}) collective-permute-start(bf16[16,16,128]{2,1,0:T(8,128)(2,1)S(1)} %assemble.1), channel_id=1, source_target_pairs={{0,48},{8,56},{16,0},{24,8},{32,16},{40,24},{48,32},{56,40},{64,11... | collective-permute-start | bytes 196616 | tf_op jit(solution)/shard_map/ppermute | solution.py:35
  28.5 3.4 %build_taps.2.t0_ref = bf16[256,64,384]{2,1,0:T(8,128)(2,1)S(1)} custom-call(s32[2]{0:T(128)S(1)} %get-tuple-element.50.live_ref, bf16[2,256,512]{2,1,0:T(8,128)(2,1)S(1)} %get-tuple-element.23.f_ref), custom_call_target="tpu_custom_call" | custom-call | flops 10000000 | bytes 14000000 | tf_op jit(solution)/shard_map/build_taps/pallas_call | solution.py:103
  32.0 0.0 collective-permute-done
  32.0 0.0 collective-permute-done.1
  32.0 0.0 collective-permute-done.2
  32.1 2.2 %collective-permute-start.4 = (bf16[64,16,128]{2,1,0:T(8,128)(2,1)S(1)}, bf16[64,16,128]{2,1,0:T(8,128)(2,1)S(1)}, u32[]{:S(2)}, u32[]{:S(2)}) collective-permute-start(bf16[64,16,128]{2,1,0:T(8,128)(2,1)S(1)} %constant_dynamic-update-slice_fusion.x_ref), channel_id=1, source_target_pairs={{0,64},{8,72},{16,80},{24,88},{32,96},{40,104},{48,112},{56,120},{... | collective-permute-start | bytes 786440 | tf_op jit(solution)/shard_map/ppermute | solution.py:35
  34.2 0.0 collective-permute-start.5
  34.2 0.1 slice_bitcast_fusion.3
  34.3 0.0 collective-permute-done.3.f_ref
  34.3 3.4 %build_taps.3.t1_ref = bf16[256,64,384]{2,1,0:T(8,128)(2,1)S(1)} custom-call(s32[2]{0:T(128)S(1)} %get-tuple-element.49.live_ref, bf16[2,256,512]{2,1,0:T(8,128)(2,1)S(1)} %collective-permute-done.3.f_ref), custom_call_target="tpu_custom_call" | custom-call | flops 10000000 | bytes 14000000 | tf_op jit(solution)/shard_map/build_taps/pallas_call | solution.py:103
  37.7 2.3 %collective-permute-start.6 = (bf16[64,16,128]{2,1,0:T(8,128)(2,1)S(1)}, bf16[64,16,128]{2,1,0:T(8,128)(2,1)S(1)}, u32[]{:S(2)}, u32[]{:S(2)}) collective-permute-start(bf16[64,16,128]{2,1,0:T(8,128)(2,1)S(1)} %constant_dynamic-update-slice_fusion.x_ref), channel_id=1, source_target_pairs={{0,128},{8,136},{16,144},{24,152},{32,160},{40,168},{48,176},{56,1... | collective-permute-start | bytes 786440 | tf_op jit(solution)/shard_map/ppermute | solution.py:35
  40.1 2.7 %detect.4 = (f32[4,256,128]{2,1,0:T(8,128)S(1)}, f32[4,8,128]{2,1,0:T(8,128)S(1)}) custom-call(s32[4]{0:T(128)S(1)} %get-tuple-element.45.piece_ref, bf16[256,64,384]{2,1,0:T(8,128)(2,1)S(1)} %build_taps.2.t0_ref, bf16[256,64,384]{2,1,0:T(8,128)(2,1)S(1)} %build_taps.3.t1_ref, bf16[64,16,128]{2,1,0:T(8,128)(2,1)S(1)} %constant_dynamic-update-slice_fusion.x_ref), custom_call_target="tpu_custom_call" | custom-call | flops 1073741824 | bytes 6291456 | tf_op jit(solution)/shard_map/detect/pallas_call | solution.py:207
  42.8 0.0 collective-permute-done.4.x_ref
  42.8 2.8 %detect.5 = (f32[4,256,128]{2,1,0:T(8,128)S(1)}, f32[4,8,128]{2,1,0:T(8,128)S(1)}) custom-call(s32[4]{0:T(128)S(1)} %get-tuple-element.48.piece_ref, bf16[256,64,384]{2,1,0:T(8,128)(2,1)S(1)} %build_taps.2.t0_ref, bf16[256,64,384]{2,1,0:T(8,128)(2,1)S(1)} %build_taps.3.t1_ref, ...), custom_call_target="tpu_custom_call", output_to_operand_aliasing={{0}: (4, {})} | custom-call | flops 1073741824 | bytes 6291456 | tf_op jit(solution)/shard_map/detect/pallas_call | solution.py:207
  45.6 1.3 %collective-permute-done.5.x_ref = bf16[64,16,128]{2,1,0:T(8,128)(2,1)S(1)} collective-permute-done((bf16[64,16,128]{2,1,0:T(8,128)(2,1)S(1)}, bf16[64,16,128]{2,1,0:T(8,128)(2,1)S(1)}, u32[]{:S(2)}, u32[]{:S(2)}) %collective-permute-start.5) | collective-permute-done | bytes 262176 | tf_op jit(solution)/shard_map/ppermute | solution.py:35
  46.9 2.7 %detect.6 = (f32[4,256,128]{2,1,0:T(8,128)S(1)}, f32[4,8,128]{2,1,0:T(8,128)S(1)}) custom-call(s32[4]{0:T(128)S(1)} %get-tuple-element.47.piece_ref, bf16[256,64,384]{2,1,0:T(8,128)(2,1)S(1)} %build_taps.2.t0_ref, bf16[256,64,384]{2,1,0:T(8,128)(2,1)S(1)} %build_taps.3.t1_ref, ...), custom_call_target="tpu_custom_call", output_to_operand_aliasing={{0}: (4, {})} | custom-call | flops 1073741824 | bytes 6291456 | tf_op jit(solution)/shard_map/detect/pallas_call | solution.py:207
  49.7 0.0 collective-permute-done.6.x_ref
  49.7 2.8 %detect.7 = (f32[4,256,128]{2,1,0:T(8,128)S(1)}, f32[4,8,128]{2,1,0:T(8,128)S(1)}) custom-call(s32[4]{0:T(128)S(1)} %get-tuple-element.46.piece_ref, bf16[256,64,384]{2,1,0:T(8,128)(2,1)S(1)} %build_taps.2.t0_ref, bf16[256,64,384]{2,1,0:T(8,128)(2,1)S(1)} %build_taps.3.t1_ref, ...), custom_call_target="tpu_custom_call", output_to_operand_aliasing={{0}: (4, {})} | custom-call | flops 1073741824 | bytes 6291456 | tf_op jit(solution)/shard_map/detect/pallas_call | solution.py:207
  52.5 0.7 collective-permute-start.7
  53.1 0.2 turn.1
  53.3 2.8 %collective-permute-done.7 = f32[2,64]{1,0:T(2,128)S(1)} collective-permute-done((f32[2,64]{1,0:T(2,128)S(1)}, f32[2,64]{1,0:T(2,128)S(1)}, u32[]{:S(2)}, u32[]{:S(2)}) %collective-permute-start.7) | collective-permute-done | bytes 544 | tf_op jit(solution)/shard_map/ppermute | solution.py:35
  56.1 0.7 collective-permute-start.10
  56.8 0.0 collective-permute-start.8
  56.8 1.1 %collective-permute-done.8 = f32[2,64]{1,0:T(2,128)S(1)} collective-permute-done((f32[2,64]{1,0:T(2,128)S(1)}, f32[2,64]{1,0:T(2,128)S(1)}, u32[]{:S(2)}, u32[]{:S(2)}) %collective-permute-start.8) | collective-permute-done | bytes 544 | tf_op jit(solution)/shard_map/ppermute | solution.py:278
  58.0 3.3 %collective-permute-start.9 = (f32[2,64]{1,0:T(2,128)S(1)}, f32[2,64]{1,0:T(2,128)S(1)}, u32[]{:S(2)}, u32[]{:S(2)}) collective-permute-start(f32[2,64]{1,0:T(2,128)S(1)} %add.66), channel_id=1, source_target_pairs={{0,2},{1,3},{2,0},{3,1},{4,6},{5,7},{6,4},{7,5},{8,10},{9,11},{10,... | collective-permute-start | bytes 1544 | tf_op jit(solution)/shard_map/ppermute | solution.py:279
  61.2 1.5 %collective-permute-done.9 = f32[2,64]{1,0:T(2,128)S(1)} collective-permute-done((f32[2,64]{1,0:T(2,128)S(1)}, f32[2,64]{1,0:T(2,128)S(1)}, u32[]{:S(2)}, u32[]{:S(2)}) %collective-permute-start.9) | collective-permute-done | bytes 544 | tf_op jit(solution)/shard_map/ppermute | solution.py:279
  62.8 0.0 collective-permute-done.10
  62.8 5.1 %collective-permute-start.11 = (f32[2,64]{1,0:T(2,128)S(1)}, f32[2,64]{1,0:T(2,128)S(1)}, u32[]{:S(2)}, u32[]{:S(2)}) collective-permute-start(f32[2,64]{1,0:T(2,128)S(1)} %add.67), channel_id=1, source_target_pairs={{0,6},{1,7},{2,4},{3,5},{4,2},{5,3},{6,0},{7,1},{8,14},{9,15},{10,... | collective-permute-start | bytes 1544 | tf_op jit(solution)/shard_map/ppermute | solution.py:281
  67.9 1.5 %collective-permute-done.11 = f32[2,64]{1,0:T(2,128)S(1)} collective-permute-done((f32[2,64]{1,0:T(2,128)S(1)}, f32[2,64]{1,0:T(2,128)S(1)}, u32[]{:S(2)}, u32[]{:S(2)}) %collective-permute-start.11) | collective-permute-done | bytes 544 | tf_op jit(solution)/shard_map/ppermute | solution.py:281
  69.4 0.8 %maximum_divide_fusion = f32[2,64,512]{2,1,0:T(8,128)} fusion(f32[2,64,256]{2,1,0:T(8,128)S(1)} %get-tuple-element.44, f32[2,64,256]{2,1,0:T(8,128)S(1)} %get-tuple-element.43, f32[2,64]{1,0:T(2,128)S(1)} %multiply_add_fusion), kind=kLoop, calls=%fused_computation.6 | loop fusion | flops 131072 | bytes 524800 | tf_op jit(solution)/shard_map/div | solution.py:287
  (13 shorter events, 0.1 us)
Async XLA Ops:
  0.0 1.0 %copy-start = (bf16[1,256,2,512]{3,2,1,0:T(2,128)(2,1)S(1)}, bf16[1,256,2,512]{3,2,1,0:T(2,128)(2,1)}, u32[]{:S(2)}) copy-start(bf16[1,256,2,512]{3,2,1,0:T(2,128)(2,1)} %param.6) | copy-start | bytes 1572868
  3.2 20.2 %all-to-all-start = ((bf16[32,16,512]{2,1,0:T(8,128)(2,1)}), bf16[32,16,512]{2,1,0:T(8,128)(2,1)S(1)}, u32[]{:S(2)}, u32[]{:S(2)}) async-start(bf16[32,16,512]{2,1,0:T(8,128)(2,1)} %bitcast.6), calls=%async_computation | async-start | bytes 1048576 | tf_op jit(solution)/shard_map/all_to_all | solution.py:257
  13.2 21.1 %collective-permute-start.3 = (bf16[2,256,512]{2,1,0:T(8,128)(2,1)S(1)}, bf16[2,256,512]{2,1,0:T(8,128)(2,1)S(1)}, u32[]{:S(2)}, u32[]{:S(2)}) collective-permute-start(bf16[2,256,512]{2,1,0:T(8,128)(2,1)S(1)} %get-tuple-element.41), channel_id=1, source_target_pairs={{0,8},{8,0},{16,24},{24,16},{32,40},{40,32},{48,56},{56,48},{64,72... | collective-permute-start | bytes 1572872 | tf_op jit(solution)/shard_map/ppermute | solution.py:35
  24.1 7.8 %collective-permute-start = (bf16[16,16,128]{2,1,0:T(8,128)(2,1)S(1)}, bf16[16,16,128]{2,1,0:T(8,128)(2,1)S(1)}, u32[]{:S(2)}, u32[]{:S(2)}) collective-permute-start(bf16[16,16,128]{2,1,0:T(8,128)(2,1)S(1)} %assemble.1), channel_id=1, source_target_pairs={{0,32},{8,40},{16,48},{24,56},{32,0},{40,8},{48,16},{56,24},{64,96... | collective-permute-start | bytes 196616 | tf_op jit(solution)/shard_map/ppermute | solution.py:35
  25.3 6.7 %collective-permute-start.1 = (bf16[16,16,128]{2,1,0:T(8,128)(2,1)S(1)}, bf16[16,16,128]{2,1,0:T(8,128)(2,1)S(1)}, u32[]{:S(2)}, u32[]{:S(2)}) collective-permute-start(bf16[16,16,128]{2,1,0:T(8,128)(2,1)S(1)} %assemble.1), channel_id=1, source_target_pairs={{0,16},{8,24},{16,32},{24,40},{32,48},{40,56},{48,0},{56,8},{64,80... | collective-permute-start | bytes 196616 | tf_op jit(solution)/shard_map/ppermute | solution.py:35
  26.0 6.0 %collective-permute-start.2 = (bf16[16,16,128]{2,1,0:T(8,128)(2,1)S(1)}, bf16[16,16,128]{2,1,0:T(8,128)(2,1)S(1)}, u32[]{:S(2)}, u32[]{:S(2)}) collective-permute-start(bf16[16,16,128]{2,1,0:T(8,128)(2,1)S(1)} %assemble.1), channel_id=1, source_target_pairs={{0,48},{8,56},{16,0},{24,8},{32,16},{40,24},{48,32},{56,40},{64,11... | collective-permute-start | bytes 196616 | tf_op jit(solution)/shard_map/ppermute | solution.py:35
  32.1 10.8 %collective-permute-start.4 = (bf16[64,16,128]{2,1,0:T(8,128)(2,1)S(1)}, bf16[64,16,128]{2,1,0:T(8,128)(2,1)S(1)}, u32[]{:S(2)}, u32[]{:S(2)}) collective-permute-start(bf16[64,16,128]{2,1,0:T(8,128)(2,1)S(1)} %constant_dynamic-update-slice_fusion.x_ref), channel_id=1, source_target_pairs={{0,64},{8,72},{16,80},{24,88},{32,96},{40,104},{48,112},{56,120},{... | collective-permute-start | bytes 786440 | tf_op jit(solution)/shard_map/ppermute | solution.py:35
  34.2 12.7 %collective-permute-start.5 = (bf16[64,16,128]{2,1,0:T(8,128)(2,1)S(1)}, bf16[64,16,128]{2,1,0:T(8,128)(2,1)S(1)}, u32[]{:S(2)}, u32[]{:S(2)}) collective-permute-start(bf16[64,16,128]{2,1,0:T(8,128)(2,1)S(1)} %constant_dynamic-update-slice_fusion.x_ref), channel_id=1, source_target_pairs={{0,192},{8,200},{16,208},{24,216},{32,224},{40,232},{48,240},{56,2... | collective-permute-start | bytes 786440 | tf_op jit(solution)/shard_map/ppermute | solution.py:35
  37.7 11.9 %collective-permute-start.6 = (bf16[64,16,128]{2,1,0:T(8,128)(2,1)S(1)}, bf16[64,16,128]{2,1,0:T(8,128)(2,1)S(1)}, u32[]{:S(2)}, u32[]{:S(2)}) collective-permute-start(bf16[64,16,128]{2,1,0:T(8,128)(2,1)S(1)} %constant_dynamic-update-slice_fusion.x_ref), channel_id=1, source_target_pairs={{0,128},{8,136},{16,144},{24,152},{32,160},{40,168},{48,176},{56,1... | collective-permute-start | bytes 786440 | tf_op jit(solution)/shard_map/ppermute | solution.py:35
  52.5 3.7 %collective-permute-start.7 = (f32[2,64]{1,0:T(2,128)S(1)}, f32[2,64]{1,0:T(2,128)S(1)}, u32[]{:S(2)}, u32[]{:S(2)}) collective-permute-start(f32[2,64]{1,0:T(2,128)S(1)} %slice.48), channel_id=1, source_target_pairs={{0,8},{8,0},{16,24},{24,16},{32,40},{40,32},{48,56},{56,48},{64,72... | collective-permute-start | bytes 1544 | tf_op jit(solution)/shard_map/ppermute | solution.py:35
  56.1 6.6 %collective-permute-start.10 = (f32[2,64,256]{2,1,0:T(8,128)S(1)}, f32[2,64,256]{2,1,0:T(8,128)S(1)}, u32[]{:S(2)}, u32[]{:S(2)}) collective-permute-start(f32[2,64,256]{2,1,0:T(8,128)S(1)} %slice.50), channel_id=1, source_target_pairs={{0,8},{8,0},{16,24},{24,16},{32,40},{40,32},{48,56},{56,48},{64,72... | collective-permute-start | bytes 393224 | tf_op jit(solution)/shard_map/ppermute | solution.py:35
  56.8 1.1 %collective-permute-start.8 = (f32[2,64]{1,0:T(2,128)S(1)}, f32[2,64]{1,0:T(2,128)S(1)}, u32[]{:S(2)}, u32[]{:S(2)}) collective-permute-start(f32[2,64]{1,0:T(2,128)S(1)} %slice_add_fusion), channel_id=1, source_target_pairs={{0,1},{1,0},{2,3},{3,2},{4,5},{5,4},{6,7},{7,6},{8,9},{9,8},{10,11... | collective-permute-start | bytes 1544 | tf_op jit(solution)/shard_map/ppermute | solution.py:278
  58.0 4.8 %collective-permute-start.9 = (f32[2,64]{1,0:T(2,128)S(1)}, f32[2,64]{1,0:T(2,128)S(1)}, u32[]{:S(2)}, u32[]{:S(2)}) collective-permute-start(f32[2,64]{1,0:T(2,128)S(1)} %add.66), channel_id=1, source_target_pairs={{0,2},{1,3},{2,0},{3,1},{4,6},{5,7},{6,4},{7,5},{8,10},{9,11},{10,... | collective-permute-start | bytes 1544 | tf_op jit(solution)/shard_map/ppermute | solution.py:279
  62.8 6.6 %collective-permute-start.11 = (f32[2,64]{1,0:T(2,128)S(1)}, f32[2,64]{1,0:T(2,128)S(1)}, u32[]{:S(2)}, u32[]{:S(2)}) collective-permute-start(f32[2,64]{1,0:T(2,128)S(1)} %add.67), channel_id=1, source_target_pairs={{0,6},{1,7},{2,4},{3,5},{4,2},{5,3},{6,0},{7,1},{8,14},{9,15},{10,... | collective-permute-start | bytes 1544 | tf_op jit(solution)/shard_map/ppermute | solution.py:281
